TPU v7x, 256 devices: a whole 4x4x8 slice. The times are simulated.
256 devices in a mesh: row: 8 (over x, core), col: 32 (over y, z).
Axes of the slice: x: 4, y: 4, z: 8, core: 2. Of those that a mesh axis runs over, the one named last changes fastest.
Arguments:
- affinity_tiles: bfloat16 [1024, 64, 128, 128], P(('row', 'col'))
- block_columns: int32 [1024, 64], P(('row', 'col')), may hold values from 0 to 127, as said below
- live_counts: int32 [8, 128], P('row', 'col'), may hold values from 1 to 64, 4096 in all within a row
- earlier_blocks: float32 [4, 64, 131072], P(None, None, ('row', 'col')), may hold values from -6 to 6
Outputs:
- new_blocks: float32 [2, 64, 131072], P(None, None, ('row', 'col'))
- triangular_factors: float32 [2, 64, 64], replicated
Inputs may be any that keep to these rules, and one draw needn't show every extreme that they name: `block_columns`: slot 0 of every block row names the block row itself; columns name block rows of the same row group. `live_counts`: slots at or past a block row's count are ignored.
All inputs are finite; a program needn't handle non-finite values.
Results may differ from a plain program's by a relative error of at most 0.0059.
Values may be sent and summed in bfloat16 or wider, within the bound.
No kernel may reach another device: no remote copies, remote signals or barrier semaphores. Data moves between devices by JAX's collectives and lax.ppermute only.
A program may use at most 64 MiB of HBM per device.

v0:
```python
import jax
import jax.numpy as jnp
from jax import lax
from jax.sharding import PartitionSpec as P

STEPS = 2


def apply_tiles(affinity_tiles, block_columns, row_counts, group_blocks):
    block_rows = affinity_tiles.shape[0]
    slot_count = affinity_tiles.shape[1]
    tile_size = affinity_tiles.shape[2]
    block_width = group_blocks.shape[0]
    slot_ids = lax.broadcasted_iota(jnp.int32, (block_rows, slot_count), 1)
    live_mask = slot_ids < row_counts[:, None]
    picked = jnp.take(group_blocks, block_columns, axis=1)
    picked = jnp.where(live_mask[None, :, :, None], picked, jnp.zeros((), jnp.bfloat16))
    running = jnp.einsum(
        "rsij,brsj->bri", affinity_tiles, picked, preferred_element_type=jnp.float32
    )
    return running.reshape(block_width, block_rows * tile_size)


def on_device(affinity_tiles, block_columns, live_counts, earlier_blocks):
    block_rows = affinity_tiles.shape[0]
    tile_size = affinity_tiles.shape[2]
    block_width = earlier_blocks.shape[1]
    rows_here = earlier_blocks.shape[2]
    total_rows = rows_here * lax.axis_size("row") * lax.axis_size("col")
    row_counts = live_counts.reshape(block_rows)
    known_list = [earlier_blocks[i] for i in range(earlier_blocks.shape[0])]
    first_half = known_list[-1].astype(jnp.bfloat16)
    group_half = lax.all_gather(first_half, "col", axis=1, tiled=True)
    fresh_list = []
    factor_list = []
    for step_index in range(STEPS):
        is_last = step_index + 1 == STEPS
        group_blocks = group_half.reshape(block_width, -1, tile_size)
        product = apply_tiles(affinity_tiles, block_columns, row_counts, group_blocks)
        known = jnp.concatenate(known_list, 0)
        local_proj = jnp.dot(known, product.T, precision=lax.Precision.HIGHEST) / total_rows
        projections = lax.psum(local_proj, ("row", "col"))
        residual = product - jnp.dot(projections.T, known, precision=lax.Precision.HIGHEST)
        local_gram = jnp.dot(residual, residual.T, precision=lax.Precision.HIGHEST) / total_rows
        gram_sum = lax.psum(local_gram, ("row", "col"))
        factor_low = jnp.linalg.cholesky(gram_sum)
        fresh = jax.scipy.linalg.solve_triangular(factor_low, residual, lower=True)
        fresh_list.append(fresh)
        factor_list.append(factor_low.T)
        known_list.append(fresh)
        if not is_last:
            group_half = lax.all_gather(fresh.astype(jnp.bfloat16), "col", axis=1, tiled=True)
    return (jnp.stack(fresh_list), jnp.stack(factor_list))


def solution(mesh):
    return jax.shard_map(
        on_device,
        mesh=mesh,
        in_specs=(
            P(("row", "col"), None, None, None),
            P(("row", "col"), None),
            P("row", "col"),
            P(None, None, ("row", "col")),
        ),
        out_specs=(P(None, None, ("row", "col")), P()),
        check_vma=False,
    )
```

profile of v0, /device:TPU:1, one launch (start us, length us, event | category | flops | bytes accessed | tf_op | source)
XLA Modules:
  0.0 864.7 jit_solution(17645085274301516106)
XLA Ops:
  7.2 1.5 fusion.32
  11.3 0.9 constant_dynamic-update-slice_fusion.3
  13.1 1.1 slice_bitcast_fusion.2
  14.3 71.6 %all-gather.3.cloned.1.call-done = bf16[64,16384]{1,0:T(8,128)(2,1)} async-done(((bf16[64,512]{1,0:T(8,128)(2,1)}), bf16[64,16384]{1,0:T(8,128)(2,1)}) %all-gather.3.cloned.1.call-update) | async-done | bytes 2097168 | tf_op jit(solution)/shard_map/all_gather | solution.py:33
  85.9 2.2 copy_bitcast_fusion.1
  88.1 3.0 gather_fusion
  91.1 6.3 fusion.12
  97.3 1.2 convolution_multiply_fusion.1
  99.6 246.5 %all-reduce.3.cloned.1.call-done = f32[256,64]{1,0:T(8,128)} async-done(((f32[256,64]{1,0:T(8,128)}), f32[256,64]{1,0:T(8,128)}) %all-reduce.3.cloned.1.call-update) | async-done | bytes 65552 | tf_op jit(solution)/shard_map/psum | solution.py:42
  346.0 1.3 convolution_subtract_fusion.1
  347.6 76.2 %psum.29 = f32[64,64]{0,1:T(8,128)S(1)} all-reduce(f32[64,64]{0,1:T(8,128)S(1)} %convolution_multiply_fusion.3), channel_id=1, replica_groups=mesh['row'=8,'col'=32] {'row','col'}, use_global_device_ids=true, to_apply=%region_1.3 | all-reduce | flops 4096 | bytes 32768 | tf_op jit(solution)/shard_map/psum | solution.py:45
  423.9 5.8 cholesky.44
  431.1 4.9 custom-call.6
  436.0 1.0 fusion.33
  437.0 66.8 %all-gather.5.cloned.1.call-done = bf16[64,16384]{1,0:T(8,128)(2,1)} async-done(((bf16[64,512]{1,0:T(8,128)(2,1)}), bf16[64,16384]{1,0:T(8,128)(2,1)}) %all-gather.5.cloned.1.call-update) | async-done | bytes 2097168 | tf_op jit(solution)/shard_map/all_gather | solution.py:52
  503.8 2.2 copy_bitcast_fusion
  506.0 3.0 gather_fusion.1
  509.0 6.3 fusion.13
  515.3 1.3 convolution_multiply_fusion
  516.7 251.0 %all-reduce.5.cloned.1.call-done = f32[320,64]{1,0:T(8,128)} async-done(((f32[320,64]{1,0:T(8,128)}), f32[320,64]{1,0:T(8,128)}) %all-reduce.5.cloned.1.call-update) | async-done | bytes 81936 | tf_op jit(solution)/shard_map/psum | solution.py:42
  767.7 1.5 convolution_subtract_fusion
  769.4 74.8 %psum.31 = f32[64,64]{0,1:T(8,128)S(1)} all-reduce(f32[64,64]{0,1:T(8,128)S(1)} %convolution_multiply_fusion.2), channel_id=1, replica_groups=mesh['row'=8,'col'=32] {'row','col'}, use_global_device_ids=true, to_apply=%region_5.9 | all-reduce | flops 4096 | bytes 32768 | tf_op jit(solution)/shard_map/psum | solution.py:45
  844.3 5.8 cholesky.55
  852.2 4.9 custom-call.7
  (31 shorter events, 9.6 us)
Async XLA Ops:
  7.2 78.7 %all-gather.3.cloned.1.call-start = ((), (), s32[]{:S(2)}) async-start(), calls=%async_computation | async-start | bytes 2162688 | tf_op jit(solution)/shard_map/all_gather | solution.py:33
  8.8 337.2 %all-reduce.3.cloned.1.call-start = ((), (), s32[]{:S(2)}) async-start(), calls=%async_computation.1 | async-start | bytes 262144 | tf_op jit(solution)/shard_map/psum | solution.py:42
  98.6 405.2 %all-gather.5.cloned.1.call-start = ((), (), s32[]{:S(2)}) async-start(), calls=%async_computation.2 | async-start | bytes 2162688 | tf_op jit(solution)/shard_map/all_gather | solution.py:52
  437.0 330.7 %all-reduce.5.cloned.1.call-start = ((), (), s32[]{:S(2)}) async-start(), calls=%async_computation.3 | async-start | bytes 327680 | tf_op jit(solution)/shard_map/psum | solution.py:42
Sparse Core Ops, SparseCore 0:
  11.0 74.8 all-gather.2
  98.7 247.2 all-reduce.2
  437.1 66.6 all-gather.4
  516.8 250.8 all-reduce.4
where the time goes:
time: 865 us
  waiting for transfers between devices  636 us (74%)
  blocking collectives  151 us (17%)
  other arithmetic  26.4 us (3%)
  matrix products  19.7 us (2%)
  local copies, waits for them, and re-layouts  17.7 us (2%)
  between operations  13.9 us (2%)
    psum x2, waiting for transfers between devices, on_device(): projections = lax.psum(local_proj, ('row', 'col'))  497 us
    psum x2, blocking collectives, on_device(): gram_sum = lax.psum(local_gram, ('row', 'col'))  151 us
    all_gather x1, waiting for transfers between devices, on_device(): group_half = lax.all_gather(first_half, 'col', axis=1, tiled=True)  71.6 us
    all_gather x1, waiting for transfers between devices, on_device(): lax.all_gather(fresh.astype(jnp.bfloat16), 'col', axis=1, tiled=True)  66.8 us
  transfers between devices with their start and end apart: 4, of which 4 were waited for; matrix products, arithmetic and copies ran while one was open for 1% of the time, Pallas kernels for 0%

commit v1 on v0

v1 whole, which is shorter than its diff:
```python
import functools

import jax
import jax.numpy as jnp
from jax import lax
from jax.experimental import pallas as pl
from jax.experimental.pallas import tpu as pltpu
from jax.sharding import PartitionSpec as P

STEPS = 2
NX, NY, NZ, NC = 4, 4, 8, 2
CHUNK = 8
HI = lax.Precision.HIGHEST


def col_id(y, z):
    return (y % NY) * NZ + z % NZ


def row_id(x, core):
    return (x % NX) * NC + core % NC


Y_UP = [(col_id(y, z), col_id(y + 1, z)) for y in range(NY) for z in range(NZ)]
Y_DOWN = [(col_id(y, z), col_id(y - 1, z)) for y in range(NY) for z in range(NZ)]
CORE_SWAP = [(row_id(x, c), row_id(x, c + 1)) for x in range(NX) for c in range(NC)]
Z_GROUPS = [[col_id(y, z) for z in range(NZ)] for y in range(NY)]
X_GROUPS = [[row_id(x, c) for x in range(NX)] for c in range(NC)]


def to_all(a, axis, count, groups=None):
    copies = jnp.broadcast_to(a[None], (count,) + a.shape)
    return lax.all_to_all(copies, axis, 0, 0, axis_index_groups=groups, tiled=True)


def gather_group(half):
    own = to_all(half, "col", NZ, Z_GROUPS)
    below = lax.ppermute(own, "col", Y_UP)
    above = lax.ppermute(own, "col", Y_DOWN)
    far_low = lax.ppermute(below[: NZ // 2], "col", Y_UP)
    far_high = lax.ppermute(above[NZ // 2 :], "col", Y_DOWN)
    everything = jnp.concatenate([own, above, far_low, far_high, below], 0)
    return everything.reshape((-1,) + half.shape[1:])


def sum_everywhere(a):
    rows = a.shape[0] // 2
    core = lax.axis_index("row") % NC
    kept = lax.dynamic_slice_in_dim(a, core * rows, rows, 0)
    sent = lax.dynamic_slice_in_dim(a, (1 - core) * rows, rows, 0)
    part = kept + lax.ppermute(sent, "row", CORE_SWAP)
    part = part.reshape(NY * NZ, rows // (NY * NZ), a.shape[1])
    piece = jnp.sum(lax.all_to_all(part, "col", 0, 0, tiled=True), 0)
    piece = jnp.sum(to_all(piece, "row", NX, X_GROUPS), 0)
    mine = to_all(piece, "col", NY * NZ).reshape(rows, a.shape[1])
    other = lax.ppermute(mine, "row", CORE_SWAP)
    first = jnp.where(core == 0, mine, other)
    second = jnp.where(core == 0, other, mine)
    return jnp.concatenate([first, second], 0)


def apply_kernel(block_rows, slots, picks, counts, group, tiles, out, store, sems):
    chunks = slots // CHUNK

    def copy(r, k):
        at = pl.ds(k * CHUNK, CHUNK)
        return pltpu.make_async_copy(tiles.at[r, at], store.at[r, at], sems.at[r, k])

    for r in range(block_rows):
        for k in range(chunks):

            @pl.when(k * CHUNK < counts[r])
            def _():
                copy(r, k).start()

    for r in range(block_rows):
        live = counts[r]

        def step(k, total):
            copy(r, k).wait()
            sides = []
            for j in range(CHUNK):
                slot = k * CHUNK + j
                side = group[picks[r * slots + slot]]
                sides.append(jnp.where(slot < live, side, jnp.zeros_like(side)))
            left = jnp.concatenate(sides, 1)
            right = jnp.concatenate([store[r, k * CHUNK + j] for j in range(CHUNK)], 1)
            return total + lax.dot_general(
                left, right, (((1,), (1,)), ((), ())), preferred_element_type=jnp.float32
            )

        width, size = group.shape[1], group.shape[2]
        total = lax.fori_loop(
            0, (live + CHUNK - 1) // CHUNK, step, jnp.zeros((width, size), jnp.float32)
        )
        out[:, r * size : (r + 1) * size] = total


def apply_tiles(tiles, picks, counts, group):
    block_rows, slots, size, _ = tiles.shape
    width = group.shape[1]
    return pl.pallas_call(
        functools.partial(apply_kernel, block_rows, slots),
        out_shape=jax.ShapeDtypeStruct((width, block_rows * size), jnp.float32),
        in_specs=[
            pl.BlockSpec(memory_space=pltpu.SMEM),
            pl.BlockSpec(memory_space=pltpu.SMEM),
            pl.BlockSpec(memory_space=pltpu.VMEM),
            pl.BlockSpec(memory_space=pl.ANY),
        ],
        out_specs=pl.BlockSpec(memory_space=pltpu.VMEM),
        scratch_shapes=[
            pltpu.VMEM((block_rows, slots, size, size), tiles.dtype),
            pltpu.SemaphoreType.DMA((block_rows, slots // CHUNK)),
        ],
        compiler_params=pltpu.CompilerParams(vmem_limit_bytes=32 << 20),
        name="apply_tiles",
    )(picks, counts, group, tiles)


def split_blocks(a, size):
    return jnp.transpose(a.reshape(a.shape[0], -1, size), (1, 0, 2))


def mm(a, b):
    return jnp.dot(a, b, precision=HI)


def pair_up(blocks):
    if len(blocks) % 2:
        blocks = blocks + [jnp.zeros_like(blocks[0])]
    rows = [jnp.concatenate(blocks[i : i + 2], 1) for i in range(0, len(blocks), 2)]
    return jnp.concatenate(rows, 0)


def unpair(a, count, b):
    return [a[i // 2 * b : (i // 2 + 1) * b, i % 2 * b : (i % 2 + 1) * b] for i in range(count)]


def on_device(tiles, block_columns, live_counts, earlier):
    block_rows, slots, size, _ = tiles.shape
    prev, b, rows_here = earlier.shape
    total_rows = rows_here * lax.axis_size("row") * lax.axis_size("col")
    counts = live_counts.reshape(block_rows)
    here_y = lax.axis_index("col") // NZ
    owner = block_columns // block_rows
    turn = (owner // NZ - here_y) % NY
    picks = (turn * NZ + owner % NZ) * block_rows + block_columns % block_rows
    picks = picks.reshape(-1)

    known = earlier.reshape(prev * b, rows_here)
    group = gather_group(split_blocks(earlier[-1].astype(jnp.bfloat16), size))
    product = apply_tiles(tiles, picks, counts, group)

    def block(a, i):
        return a[i * b : (i + 1) * b]

    stack = jnp.concatenate([known, product], 0)
    inner = mm(stack, stack.T) / total_rows
    pairs = [(i, j) for i in range(prev + 1) for j in range(i, prev + 1)]
    blocks = [inner[i * b : (i + 1) * b, j * b : (j + 1) * b] for i, j in pairs]
    sums = unpair(sum_everywhere(pair_up(blocks)), len(blocks), b)
    table = dict(zip(pairs, sums))
    proj = jnp.concatenate([table[i, prev] for i in range(prev)], 0)
    own = jnp.concatenate(
        [
            jnp.concatenate(
                [table[i, j] if i <= j else table[j, i].T for j in range(prev)], 1
            )
            for i in range(prev)
        ],
        0,
    )
    spread = mm(own, proj)
    gram = table[prev, prev] + mm(proj.T, spread - 2 * proj)
    residual = product - mm(proj.T, known)
    factor = jnp.linalg.cholesky(gram)
    eye = jnp.eye(b, dtype=jnp.float32)
    inverse = jax.scipy.linalg.solve_triangular(factor, eye, lower=True)
    fresh = mm(inverse, residual)
    factors = [factor.T]
    fresh_list = [fresh]

    group = gather_group(split_blocks(fresh.astype(jnp.bfloat16), size))
    product = apply_tiles(tiles, picks, counts, group)
    known = jnp.concatenate([known, fresh], 0)
    stack = jnp.concatenate([known, product], 0)
    inner = mm(stack, product.T) / total_rows
    blocks = [block(inner, i) for i in range(prev + 2)]
    blocks += [jnp.zeros_like(blocks[0])] * (16 - len(blocks))
    sums = unpair(sum_everywhere(pair_up(blocks)), prev + 2, b)
    proj2 = jnp.concatenate(sums[: prev + 1], 0)
    cross = mm(proj - spread, inverse.T)
    top = jnp.concatenate([own, cross], 1)
    low = jnp.concatenate([cross.T, eye], 1)
    spread2 = mm(jnp.concatenate([top, low], 0), proj2)
    gram = sums[prev + 1] + mm(proj2.T, spread2 - 2 * proj2)
    residual = product - mm(proj2.T, known)
    factor = jnp.linalg.cholesky(gram)
    fresh_list.append(jax.scipy.linalg.solve_triangular(factor, residual, lower=True))
    factors.append(factor.T)
    return (jnp.stack(fresh_list), jnp.stack(factors))


def solution(mesh):
    return jax.shard_map(
        on_device,
        mesh=mesh,
        in_specs=(
            P(("row", "col"), None, None, None),
            P(("row", "col"), None),
            P("row", "col"),
            P(None, None, ("row", "col")),
        ),
        out_specs=(P(None, None, ("row", "col")), P()),
        check_vma=False,
    )
```

time: 865 us -> 232 us (0.27)
  waiting for transfers between devices: 636 us -> 42.1 us
  blocking collectives: 151 us -> 100 us
  starting transfers between devices: 0.16 us -> 34.2 us
  matrix products: 19.7 us -> 5.87 us
  between operations: 13.9 us -> 1.23 us
  Pallas kernels: 0 us -> 9.67 us
    psum x2 -> x0, waiting for transfers between devices: 497 us -> none  [on_device(): projections = lax.psum(local_proj, ('row', 'col'))]
    psum x2 -> x0, blocking collectives: 151 us -> none  [on_device(): gram_sum = lax.psum(local_gram, ('row', 'col'))]
    all_gather x2 -> x0, waiting for transfers between devices: 138 us -> none  [the longest x1 71.6 us: on_device(): group_half = lax.all_gather(first_half, 'col', axis=1, tiled=True)]
    all_to_all x0 -> x7, blocking collectives: none -> 100 us  [the longest x5 73 us: to_all(): lax.all_to_all(copies, axis, 0, 0, axis_index_groups=groups, tiled=True)]
    ppermute x0 -> x12, waiting for transfers between devices: none -> 33 us  [the longest x2 21.3 us: gather_group(): below = lax.ppermute(own, 'col', Y_UP)]
    ppermute x0 -> x12, starting transfers between devices: none -> 29.8 us  [the longest x2 10.3 us: sum_everywhere(): part = kept + lax.ppermute(sent, 'row', CORE_SWAP)]
    dot_general x8 -> x10, matrix products: 18.4 us -> 5.3 us  [mm(): return jnp.dot(a, b, precision=HI)]
    pallas_call x0 -> x2, Pallas kernels: none -> 9.67 us  [apply_tiles(): pl.pallas_call(functools.partial(apply_kernel, block_rows, slots), out_sh...]
  transfers between devices with their start and end apart: 4 -> 13, of which waited for: 4 -> 9; matrix products, arithmetic and copies ran while one was open for 1% -> 0% of each run, Pallas kernels for 0% -> 0%
where the time goes in v1:
time: 232 us; the launch traced here: 231 us
  blocking collectives  100 us (43%)
  waiting for transfers between devices  42.1 us (18%)
  starting transfers between devices  34.2 us (15%)
  other arithmetic  25.3 us (11%)
  local copies, waits for them, and re-layouts  12.2 us (5%)
  Pallas kernels  9.67 us (4%)
  matrix products  5.87 us (3%)
    all_to_all x5, blocking collectives, to_all(): lax.all_to_all(copies, axis, 0, 0, axis_index_groups=groups, tiled=True)  73 us
    all_to_all x2, blocking collectives, sum_everywhere(): piece = jnp.sum(lax.all_to_all(part, 'col', 0, 0, tiled=True), 0)  27.2 us
    ppermute x2, waiting for transfers between devices, gather_group(): below = lax.ppermute(own, 'col', Y_UP)  21.3 us
    another operation x6, other arithmetic, on_device(): factor = jnp.linalg.cholesky(gram)  13 us
    ppermute x2, starting transfers between devices, sum_everywhere(): part = kept + lax.ppermute(sent, 'row', CORE_SWAP)  10.3 us
    pallas_call x2, Pallas kernels, apply_tiles(): pl.pallas_call(functools.partial(apply_kernel, block_rows, slots), out_sh...  9.67 us
    all_to_all x1, waiting for transfers between devices, to_all(): lax.all_to_all(copies, axis, 0, 0, axis_index_groups=groups, tiled=True)  9.14 us
    ppermute x2, starting transfers between devices, sum_everywhere(): other = lax.ppermute(mine, 'row', CORE_SWAP)  8.43 us
  transfers between devices with their start and end apart: 13, of which 9 were waited for; matrix products, arithmetic and copies ran while one was open for 0% of the time, Pallas kernels for 0%

profile of v1, /device:TPU:1, one launch (start us, length us, event | category | flops | bytes accessed | tf_op | source)
XLA Modules:
  0.0 230.7 jit_solution(13884352568168634306)
XLA Ops:
  1.7 24.9 %all_to_all.40 = bf16[8,4,64,128]{3,2,1,0:T(8,128)(2,1)S(1)} all-to-all(bf16[8,4,64,128]{3,2,1,0:T(8,128)(2,1)S(1)} %broadcast_in_dim.15), channel_id=1, replica_groups={{0,1,2,3,4,5,6,7},{8,9,10,11,12,13,14,15},{16,17,18,19,20,21,22,23},{24..., dimensions={0} | all-to-all | bytes 1048576 | tf_op jit(solution)/shard_map/all_to_all | solution.py:33
  29.4 9.7 %collective-permute-done.1 = bf16[8,4,64,128]{3,2,1,0:T(8,128)(2,1)S(1)} collective-permute-done((bf16[8,4,64,128]{3,2,1,0:T(8,128)(2,1)S(1)}, bf16[8,4,64,128]{3,2,1,0:T(8,128)(2,1)S(1)}, u32[]{:S(2)}, u32[]{:S(2)}) %collective-permute-start.1) | collective-permute-done | bytes 524320 | tf_op jit(solution)/shard_map/ppermute | solution.py:38
  42.3 3.4 %collective-permute-done.2 = bf16[4,4,64,128]{3,2,1,0:T(8,128)(2,1)S(1)} collective-permute-done((bf16[4,4,64,128]{3,2,1,0:T(8,128)(2,1)S(1)}, bf16[4,4,64,128]{3,2,1,0:T(8,128)(2,1)S(1)}, u32[]{:S(2)}, u32[]{:S(2)}) %collective-permute-start.2) | collective-permute-done | bytes 262176 | tf_op jit(solution)/shard_map/ppermute | solution.py:40
  45.8 3.4 %copy-done = bf16[4,64,128,128]{3,2,1,0:T(8,128)(2,1)S(1)} copy-done((bf16[4,64,128,128]{3,2,1,0:T(8,128)(2,1)S(1)}, bf16[4,64,128,128]{3,2,1,0:T(8,128)(2,1)}, u32[]{:S(2)}) %copy-start) | copy-done | bytes 8388632
  49.2 4.8 %apply_tiles.2 = f32[64,512]{1,0:T(8,128)S(1)} custom-call(s32[256]{0:T(256)S(1)} %reshape.57.picks, s32[4]{0:T(128)S(1)} %bitcast.67, bf16[128,64,128]{2,1,0:T(8,128)(2,1)S(1)} %bitcast.65, bf16[4,64,128,128]{3,2,1,0:T(8,128)(2,1)S(1)} %copy-done), custom_call_target="tpu_custom_call" | custom-call | tf_op jit(solution)/shard_map/apply_tiles/pallas_call | solution.py:102
  55.7 6.2 %collective-permute-start.4 = (f32[256,128]{1,0:T(8,128)S(1)}, f32[256,128]{1,0:T(8,128)S(1)}, u32[]{:S(2)}, u32[]{:S(2)}) collective-permute-start(f32[256,128]{1,0:T(8,128)S(1)} %constant_dynamic-slice_fusion.1), channel_id=1, source_target_pairs={{0,32},{32,0},{64,96},{96,64},{128,160},{160,128},{192,224},{224,1... | collective-permute-start | bytes 393224 | tf_op jit(solution)/shard_map/ppermute | solution.py:51
  62.9 14.6 %all_to_all.41 = f32[32,8,128]{2,1,0:T(8,128)S(1)} all-to-all(f32[32,8,128]{2,1,0:T(8,128)S(1)} %add_bitcast_fusion.1), channel_id=1, replica_groups=mesh['row'=8,'col'=32] {'col'}, dimensions={0} | all-to-all | bytes 262144 | tf_op jit(solution)/shard_map/all_to_all | solution.py:53
  77.5 7.8 %all_to_all.42 = f32[4,8,128]{2,1,0:T(8,128)S(1)} all-to-all(f32[4,8,128]{2,1,0:T(8,128)S(1)} %broadcast_in_dim.16), channel_id=1, replica_groups={{0,64,128,192},{32,96,160,224},{1,65,129,193},{33,97,161,225},{2,66,130..., dimensions={0} | all-to-all | bytes 32768 | tf_op jit(solution)/shard_map/all_to_all | solution.py:33
  85.3 13.3 %all_to_all.43 = f32[32,8,128]{2,1,0:T(8,128)S(1)} all-to-all(f32[32,8,128]{2,1,0:T(8,128)S(1)} %broadcast_in_dim.17), channel_id=1, replica_groups=mesh['row'=8,'col'=32] {'col'}, dimensions={0} | all-to-all | bytes 262144 | tf_op jit(solution)/shard_map/all_to_all | solution.py:33
  98.6 4.1 %collective-permute-start.5 = (f32[256,128]{1,0:T(8,128)S(1)}, f32[256,128]{1,0:T(8,128)S(1)}, u32[]{:S(2)}, u32[]{:S(2)}) collective-permute-start(f32[256,128]{1,0:T(8,128)S(1)} %bitcast.73), channel_id=1, source_target_pairs={{0,32},{32,0},{64,96},{96,64},{128,160},{160,128},{192,224},{224,1... | collective-permute-start | bytes 393224 | tf_op jit(solution)/shard_map/ppermute | solution.py:56
  106.1 5.9 %cholesky.44 = f32[64,64]{1,0:T(8,128)S(1)} custom-call(f32[64,64]{1,0:T(8,128)S(1)} %copy.64), custom_call_target="Cholesky" | custom-call | tf_op jit(solution)/shard_map/jit(cholesky)/cholesky | solution.py:177
  113.3 4.9 %custom-call.10 = f32[1,64,64]{1,2,0:T(8,128)S(1)} custom-call(f32[1,64,64]{2,1,0:T(8,128)S(1)} %get-tuple-element.41), custom_call_target="InvertDiagBlocksLowerTriangular" | custom-call | tf_op jit(solution)/shard_map/jit(_solve_triangular)/triangular_solve | solution.py:179
  118.9 20.4 %all_to_all.44 = bf16[8,4,64,128]{3,2,1,0:T(8,128)(2,1)S(1)} all-to-all(bf16[8,4,64,128]{3,2,1,0:T(8,128)(2,1)S(1)} %broadcast_in_dim.19), channel_id=1, replica_groups={{0,1,2,3,4,5,6,7},{8,9,10,11,12,13,14,15},{16,17,18,19,20,21,22,23},{24..., dimensions={0} | all-to-all | bytes 1048576 | tf_op jit(solution)/shard_map/all_to_all | solution.py:33
  141.9 11.5 %collective-permute-done.7 = bf16[8,4,64,128]{3,2,1,0:T(8,128)(2,1)S(1)} collective-permute-done((bf16[8,4,64,128]{3,2,1,0:T(8,128)(2,1)S(1)}, bf16[8,4,64,128]{3,2,1,0:T(8,128)(2,1)S(1)}, u32[]{:S(2)}, u32[]{:S(2)}) %collective-permute-start.7) | collective-permute-done | bytes 524320 | tf_op jit(solution)/shard_map/ppermute | solution.py:38
  156.5 4.8 %collective-permute-done.8 = bf16[4,4,64,128]{3,2,1,0:T(8,128)(2,1)S(1)} collective-permute-done((bf16[4,4,64,128]{3,2,1,0:T(8,128)(2,1)S(1)}, bf16[4,4,64,128]{3,2,1,0:T(8,128)(2,1)S(1)}, u32[]{:S(2)}, u32[]{:S(2)}) %collective-permute-start.8) | collective-permute-done | bytes 262176 | tf_op jit(solution)/shard_map/ppermute | solution.py:40
  164.9 4.8 %apply_tiles.3 = f32[64,512]{1,0:T(8,128)S(1)} custom-call(s32[256]{0:T(256)S(1)} %reshape.57.picks, s32[4]{0:T(128)S(1)} %bitcast.68, bf16[128,64,128]{2,1,0:T(8,128)(2,1)S(1)} %bitcast.66, bf16[4,64,128,128]{3,2,1,0:T(8,128)(2,1)S(1)} %copy-done.1), custom_call_target="tpu_custom_call" | custom-call | tf_op jit(solution)/shard_map/apply_tiles/pallas_call | solution.py:102
  171.0 4.1 %collective-permute-start.10 = (f32[256,128]{1,0:T(8,128)S(1)}, f32[256,128]{1,0:T(8,128)S(1)}, u32[]{:S(2)}, u32[]{:S(2)}) collective-permute-start(f32[256,128]{1,0:T(8,128)S(1)} %constant_dynamic-slice_fusion), channel_id=1, source_target_pairs={{0,32},{32,0},{64,96},{96,64},{128,160},{160,128},{192,224},{224,1... | collective-permute-start | bytes 393224 | tf_op jit(solution)/shard_map/ppermute | solution.py:51
  176.2 12.7 %all_to_all.45 = f32[32,8,128]{2,1,0:T(8,128)S(1)} all-to-all(f32[32,8,128]{2,1,0:T(8,128)S(1)} %add_bitcast_fusion), channel_id=1, replica_groups=mesh['row'=8,'col'=32] {'col'}, dimensions={0} | all-to-all | bytes 262144 | tf_op jit(solution)/shard_map/all_to_all | solution.py:53
  188.9 6.6 %all_to_all.46 = f32[4,8,128]{2,1,0:T(8,128)S(1)} all-to-all(f32[4,8,128]{2,1,0:T(8,128)S(1)} %broadcast_in_dim.20), channel_id=1, replica_groups={{0,64,128,192},{32,96,160,224},{1,65,129,193},{33,97,161,225},{2,66,130..., dimensions={0} | all-to-all | bytes 32768 | tf_op jit(solution)/shard_map/all_to_all | solution.py:33
  196.1 4.4 %all-to-all-start.7 = ((f32[32,8,128]{2,1,0:T(8,128)}), f32[32,8,128]{2,1,0:T(8,128)S(1)}, u32[]{:S(2)}, u32[]{:S(2)}) async-start(f32[32,8,128]{2,1,0:T(8,128)} %broadcast_in_dim.21), calls=%async_computation.7 | async-start | bytes 262144 | tf_op jit(solution)/shard_map/all_to_all | solution.py:33
  200.5 9.1 %all-to-all-done.7 = f32[32,8,128]{2,1,0:T(8,128)S(1)} async-done(((f32[32,8,128]{2,1,0:T(8,128)}), f32[32,8,128]{2,1,0:T(8,128)S(1)}, u32[]{:S(2)}, u32[]{:S(2)}) %all-to-all-start.7) | async-done | bytes 131104 | tf_op jit(solution)/shard_map/all_to_all | solution.py:33
  209.7 4.3 %collective-permute-start.11 = (f32[256,128]{0,1:T(8,128)S(1)}, f32[256,128]{0,1:T(8,128)S(1)}, u32[]{:S(2)}, u32[]{:S(2)}) collective-permute-start(f32[256,128]{0,1:T(8,128)S(1)} %copy.70), channel_id=1, source_target_pairs={{0,32},{32,0},{64,96},{96,64},{128,160},{160,128},{192,224},{224,1... | collective-permute-start | bytes 393224 | tf_op jit(solution)/shard_map/ppermute | solution.py:56
  216.8 5.8 %cholesky.55 = f32[64,64]{1,0:T(8,128)S(1)} custom-call(f32[64,64]{1,0:T(8,128)S(1)} %fusion.71), custom_call_target="Cholesky" | custom-call | tf_op jit(solution)/shard_map/jit(cholesky)/cholesky | solution.py:199
  224.7 4.9 %custom-call.11 = f32[1,64,64]{1,2,0:T(8,128)S(1)} custom-call(f32[1,64,64]{2,1,0:T(8,128)S(1)} %get-tuple-element.43), custom_call_target="InvertDiagBlocksLowerTriangular" | custom-call | tf_op jit(solution)/shard_map/jit(_solve_triangular)/triangular_solve | solution.py:200
  (125 shorter events, 33.0 us)
Async XLA Ops:
  0.6 38.6 %copy-start.4 = (s32[4,64]{1,0:T(4,128)S(1)}, s32[4,64]{1,0:T(4,128)}, u32[]{:S(2)}) copy-start(s32[4,64]{1,0:T(4,128)} %param.6) | copy-start | bytes 3076
  26.6 12.5 %collective-permute-start.1 = (bf16[8,4,64,128]{3,2,1,0:T(8,128)(2,1)S(1)}, bf16[8,4,64,128]{3,2,1,0:T(8,128)(2,1)S(1)}, u32[]{:S(2)}, u32[]{:S(2)}) collective-permute-start(bf16[8,4,64,128]{3,2,1,0:T(8,128)(2,1)S(1)} %all_to_all.40), channel_id=1, source_target_pairs={{0,8},{1,9},{2,10},{3,11},{4,12},{5,13},{6,14},{7,15},{8,16},{9,17... | collective-permute-start | bytes 1572872 | tf_op jit(solution)/shard_map/ppermute | solution.py:38
  27.9 11.4 %collective-permute-start = (bf16[8,4,64,128]{3,2,1,0:T(8,128)(2,1)S(1)}, bf16[8,4,64,128]{3,2,1,0:T(8,128)(2,1)S(1)}, u32[]{:S(2)}, u32[]{:S(2)}) collective-permute-start(bf16[8,4,64,128]{3,2,1,0:T(8,128)(2,1)S(1)} %all_to_all.40), channel_id=1, source_target_pairs={{0,24},{1,25},{2,26},{3,27},{4,28},{5,29},{6,30},{7,31},{8,0},{9,1... | collective-permute-start | bytes 1572872 | tf_op jit(solution)/shard_map/ppermute | solution.py:39
  39.1 6.5 %collective-permute-start.2 = (bf16[4,4,64,128]{3,2,1,0:T(8,128)(2,1)S(1)}, bf16[4,4,64,128]{3,2,1,0:T(8,128)(2,1)S(1)}, u32[]{:S(2)}, u32[]{:S(2)}) collective-permute-start(bf16[4,4,64,128]{3,2,1,0:T(8,128)(2,1)S(1)} %slice.189), channel_id=1, source_target_pairs={{0,8},{1,9},{2,10},{3,11},{4,12},{5,13},{6,14},{7,15},{8,16},{9,17... | collective-permute-start | bytes 786440 | tf_op jit(solution)/shard_map/ppermute | solution.py:40
  39.4 6.4 %copy-start.2 = (s32[1,4]{1,0:T(1,128)S(1)}, s32[1,4]{1,0:T(1,128)}, u32[]{:S(2)}) copy-start(s32[1,4]{1,0:T(1,128)} %param.7) | copy-start | bytes 52
  39.4 6.3 %collective-permute-start.3 = (bf16[4,4,64,128]{3,2,1,0:T(8,128)(2,1)S(1)}, bf16[4,4,64,128]{3,2,1,0:T(8,128)(2,1)S(1)}, u32[]{:S(2)}, u32[]{:S(2)}) collective-permute-start(bf16[4,4,64,128]{3,2,1,0:T(8,128)(2,1)S(1)} %slice.190), channel_id=1, source_target_pairs={{0,24},{1,25},{2,26},{3,27},{4,28},{5,29},{6,30},{7,31},{8,0},{9,1... | collective-permute-start | bytes 786440 | tf_op jit(solution)/shard_map/ppermute | solution.py:41
  45.8 3.4 %copy-start = (bf16[4,64,128,128]{3,2,1,0:T(8,128)(2,1)S(1)}, bf16[4,64,128,128]{3,2,1,0:T(8,128)(2,1)}, u32[]{:S(2)}) copy-start(bf16[4,64,128,128]{3,2,1,0:T(8,128)(2,1)} %tiles.3) | copy-start | bytes 25165828
  49.2 4.8 %copy-start.3 = (f32[4,64,512]{2,1,0:T(8,128)S(1)}, f32[4,64,512]{2,1,0:T(8,128)}, u32[]{:S(2)}) copy-start(f32[4,64,512]{2,1,0:T(8,128)} %param.8) | copy-start | bytes 1572868
  55.7 7.2 %collective-permute-start.4 = (f32[256,128]{1,0:T(8,128)S(1)}, f32[256,128]{1,0:T(8,128)S(1)}, u32[]{:S(2)}, u32[]{:S(2)}) collective-permute-start(f32[256,128]{1,0:T(8,128)S(1)} %constant_dynamic-slice_fusion.1), channel_id=1, source_target_pairs={{0,32},{32,0},{64,96},{96,64},{128,160},{160,128},{192,224},{224,1... | collective-permute-start | bytes 393224 | tf_op jit(solution)/shard_map/ppermute | solution.py:51
  98.6 5.1 %collective-permute-start.5 = (f32[256,128]{1,0:T(8,128)S(1)}, f32[256,128]{1,0:T(8,128)S(1)}, u32[]{:S(2)}, u32[]{:S(2)}) collective-permute-start(f32[256,128]{1,0:T(8,128)S(1)} %bitcast.73), channel_id=1, source_target_pairs={{0,32},{32,0},{64,96},{96,64},{128,160},{160,128},{192,224},{224,1... | collective-permute-start | bytes 393224 | tf_op jit(solution)/shard_map/ppermute | solution.py:56
  139.3 14.2 %collective-permute-start.7 = (bf16[8,4,64,128]{3,2,1,0:T(8,128)(2,1)S(1)}, bf16[8,4,64,128]{3,2,1,0:T(8,128)(2,1)S(1)}, u32[]{:S(2)}, u32[]{:S(2)}) collective-permute-start(bf16[8,4,64,128]{3,2,1,0:T(8,128)(2,1)S(1)} %all_to_all.44), channel_id=1, source_target_pairs={{0,8},{1,9},{2,10},{3,11},{4,12},{5,13},{6,14},{7,15},{8,16},{9,17... | collective-permute-start | bytes 1572872 | tf_op jit(solution)/shard_map/ppermute | solution.py:38
  139.6 14.0 %collective-permute-start.6 = (bf16[8,4,64,128]{3,2,1,0:T(8,128)(2,1)S(1)}, bf16[8,4,64,128]{3,2,1,0:T(8,128)(2,1)S(1)}, u32[]{:S(2)}, u32[]{:S(2)}) collective-permute-start(bf16[8,4,64,128]{3,2,1,0:T(8,128)(2,1)S(1)} %all_to_all.44), channel_id=1, source_target_pairs={{0,24},{1,25},{2,26},{3,27},{4,28},{5,29},{6,30},{7,31},{8,0},{9,1... | collective-permute-start | bytes 1572872 | tf_op jit(solution)/shard_map/ppermute | solution.py:39
  153.5 7.8 %collective-permute-start.8 = (bf16[4,4,64,128]{3,2,1,0:T(8,128)(2,1)S(1)}, bf16[4,4,64,128]{3,2,1,0:T(8,128)(2,1)S(1)}, u32[]{:S(2)}, u32[]{:S(2)}) collective-permute-start(bf16[4,4,64,128]{3,2,1,0:T(8,128)(2,1)S(1)} %slice.212), channel_id=1, source_target_pairs={{0,8},{1,9},{2,10},{3,11},{4,12},{5,13},{6,14},{7,15},{8,16},{9,17... | collective-permute-start | bytes 786440 | tf_op jit(solution)/shard_map/ppermute | solution.py:40
  153.6 7.7 %collective-permute-start.9 = (bf16[4,4,64,128]{3,2,1,0:T(8,128)(2,1)S(1)}, bf16[4,4,64,128]{3,2,1,0:T(8,128)(2,1)S(1)}, u32[]{:S(2)}, u32[]{:S(2)}) collective-permute-start(bf16[4,4,64,128]{3,2,1,0:T(8,128)(2,1)S(1)} %slice.213), channel_id=1, source_target_pairs={{0,24},{1,25},{2,26},{3,27},{4,28},{5,29},{6,30},{7,31},{8,0},{9,1... | collective-permute-start | bytes 786440 | tf_op jit(solution)/shard_map/ppermute | solution.py:41
  161.5 3.4 %copy-start.1 = (bf16[4,64,128,128]{3,2,1,0:T(8,128)(2,1)S(1)}, bf16[4,64,128,128]{3,2,1,0:T(8,128)(2,1)}, u32[]{:S(2)}) copy-start(bf16[4,64,128,128]{3,2,1,0:T(8,128)(2,1)} %tiles.3) | copy-start | bytes 25165828
  171.0 5.1 %collective-permute-start.10 = (f32[256,128]{1,0:T(8,128)S(1)}, f32[256,128]{1,0:T(8,128)S(1)}, u32[]{:S(2)}, u32[]{:S(2)}) collective-permute-start(f32[256,128]{1,0:T(8,128)S(1)} %constant_dynamic-slice_fusion), channel_id=1, source_target_pairs={{0,32},{32,0},{64,96},{96,64},{128,160},{160,128},{192,224},{224,1... | collective-permute-start | bytes 393224 | tf_op jit(solution)/shard_map/ppermute | solution.py:51
  196.1 13.5 %all-to-all-start.7 = ((f32[32,8,128]{2,1,0:T(8,128)}), f32[32,8,128]{2,1,0:T(8,128)S(1)}, u32[]{:S(2)}, u32[]{:S(2)}) async-start(f32[32,8,128]{2,1,0:T(8,128)} %broadcast_in_dim.21), calls=%async_computation.7 | async-start | bytes 262144 | tf_op jit(solution)/shard_map/all_to_all | solution.py:33
  209.7 5.3 %collective-permute-start.11 = (f32[256,128]{0,1:T(8,128)S(1)}, f32[256,128]{0,1:T(8,128)S(1)}, u32[]{:S(2)}, u32[]{:S(2)}) collective-permute-start(f32[256,128]{0,1:T(8,128)S(1)} %copy.70), channel_id=1, source_target_pairs={{0,32},{32,0},{64,96},{96,64},{128,160},{160,128},{192,224},{224,1... | collective-permute-start | bytes 393224 | tf_op jit(solution)/shard_map/ppermute | solution.py:56

commit v2 on v0

v2 whole, which is shorter than its diff:
```python
import functools

import jax
import jax.numpy as jnp
from jax import lax
from jax.experimental import pallas as pl
from jax.experimental.pallas import tpu as pltpu
from jax.sharding import PartitionSpec as P

STEPS = 2
NX, NY, NZ, NC = 4, 4, 8, 2
SUB = 8
GROUP = 4
AT_ONCE = 4
FAR = 2
VECTORS = 32
CODE = 128
DEAD = CODE - 1
HI = lax.Precision.HIGHEST


def col_id(y, z):
    return (y % NY) * NZ + z % NZ


def row_id(x, core):
    return (x % NX) * NC + core % NC


Y_UP = [(col_id(y, z), col_id(y + 1, z)) for y in range(NY) for z in range(NZ)]
Y_DOWN = [(col_id(y, z), col_id(y - 1, z)) for y in range(NY) for z in range(NZ)]
Z_GROUPS = [[col_id(y, z) for z in range(NZ)] for y in range(NY)]
XY_GROUPS = [
    [row_id(x, c) * NY * NZ + col_id(y, z) for x in range(NX) for y in range(NY)]
    for c in range(NC)
    for z in range(NZ)
]
CZ_GROUPS = [
    [row_id(x, c) * NY * NZ + col_id(y, z) for c in range(NC) for z in range(NZ)]
    for x in range(NX)
    for y in range(NY)
]
ALL = ("row", "col")


def to_all(a, axis, count, groups=None):
    copies = jnp.broadcast_to(a[None], (count,) + a.shape)
    return lax.all_to_all(copies, axis, 0, 0, axis_index_groups=groups, tiled=True)


def gather_group(half):
    own = to_all(half, "col", NZ, Z_GROUPS)
    below = lax.ppermute(own, "col", Y_UP)
    above = lax.ppermute(own, "col", Y_DOWN)
    far_low = lax.ppermute(below[: NZ // 2], "col", Y_UP)
    far_high = lax.ppermute(above[NZ // 2 :], "col", Y_DOWN)
    return own, above, far_low, far_high, below


def sum_everywhere(a):
    members = NX * NY
    part = a.reshape(members, a.shape[0] // members, a.shape[1])
    piece = lax.all_to_all(part, ALL, 0, 0, axis_index_groups=XY_GROUPS, tiled=True)
    piece = jnp.sum(piece, 0)
    piece = jnp.sum(to_all(piece, ALL, NC * NZ, CZ_GROUPS), 0)
    return to_all(piece, ALL, members, XY_GROUPS).reshape(a.shape)


def dot_nt(a, b):
    return lax.dot_general(
        a, b, (((1,), (1,)), ((), ())), precision=HI, preferred_element_type=jnp.float32
    )


def dot_nn(a, b):
    return lax.dot_general(
        a, b, (((1,), (0,)), ((), ())), precision=HI, preferred_element_type=jnp.float32
    )


def prepare_kernel(slots, picks, counts, near, near_rows, far, far_rows, totals):
    block_rows = counts.shape[0]

    def sort(r, carry):
        def one(s, carry):
            a, f = carry
            pick = picks[r * slots + s]
            turn = pick // VECTORS
            beyond = (turn == FAR).astype(jnp.int32)
            after = (turn > FAR).astype(jnp.int32)
            near[a] = s * CODE + pick - after * VECTORS
            far[f] = s * CODE + pick - FAR * VECTORS
            return a + 1 - beyond, f + beyond

        def fill(table, rows, start, end):
            for j in range(GROUP):
                table[end + j] = DEAD
            stop = (end + GROUP - 1) // GROUP

            def mark(c, _):
                rows[c] = r
                return 0

            lax.fori_loop(start // GROUP, stop, mark, 0)
            return stop * GROUP

        a, f = lax.fori_loop(0, counts[r], one, carry)
        return fill(near, near_rows, carry[0], a), fill(far, far_rows, carry[1], f)

    a, f = lax.fori_loop(0, block_rows, sort, (jnp.int32(0), jnp.int32(0)))
    for n, (table, rows, end) in enumerate(((near, near_rows, a), (far, far_rows, f))):
        for j in range(GROUP * AT_ONCE):
            table[end + j] = DEAD
        for j in range(AT_ONCE):
            rows[end // GROUP + j] = 0
        totals[n] = (end + GROUP * AT_ONCE - 1) // (GROUP * AT_ONCE)


def prepare(tiles, picks, counts):
    block_rows, slots = tiles.shape[:2]
    smem = pl.BlockSpec(memory_space=pltpu.SMEM)
    entries = block_rows * (slots + GROUP) + 2 * GROUP * AT_ONCE
    table = jax.ShapeDtypeStruct((entries,), jnp.int32)
    rows = jax.ShapeDtypeStruct((entries // GROUP,), jnp.int32)
    return pl.pallas_call(
        functools.partial(prepare_kernel, slots),
        out_shape=(
            table,
            rows,
            table,
            rows,
            jax.ShapeDtypeStruct((2,), jnp.int32),
        ),
        in_specs=[smem, smem],
        out_specs=(smem,) * 5,
        compiler_params=pltpu.CompilerParams(vmem_limit_bytes=16 << 20),
        cost_estimate=pl.CostEstimate(flops=0, bytes_accessed=8 << 20, transcendentals=0),
        name="prepare",
    )(picks, counts)


def multiply(table, rows, trips, parts, store, group, sems, total):
    copies, start = [], 0
    for n, part in enumerate(parts):
        at = pl.ds(start, part.shape[0])
        copies.append(pltpu.make_async_copy(part, group.at[at], sems.at[n]))
        start += part.shape[0]
    for c in copies:
        c.start()
    group[start] = jnp.zeros(group.shape[1:], group.dtype)
    for c in copies:
        c.wait()
    block_rows = group.shape[1]
    dead = start * block_rows

    def step(t, carry):
        for c in range(AT_ONCE):
            chunk = t * AT_ONCE + c
            r = rows[chunk]
            left, right = [], []
            for j in range(GROUP):
                code = table[chunk * GROUP + j]
                pick = jnp.minimum(code % CODE, dead)
                left.append(group[pick // block_rows, pick % block_rows])
                right.append(store[r, code // CODE])
            total[r] += lax.dot_general(
                jnp.concatenate(left, 1),
                jnp.concatenate(right, 1),
                (((1,), (1,)), ((), ())),
                preferred_element_type=jnp.float32,
            )
        return carry

    lax.fori_loop(0, trips, step, 0)


def near_kernel(table, rows, totals, own, above, below, store, total, group, sems):
    total[...] = jnp.zeros_like(total)
    multiply(table, rows, totals[0], (own, above, below), store, group, sems, total)


def far_kernel(scale, table, rows, totals, low, high, store, start, known, *refs):
    out, inner, group, sems, total = refs
    total[...] = start[...]
    multiply(table, rows, totals[1], (low, high), store, group, sems, total)
    product = jnp.concatenate([total[r] for r in range(total.shape[0])], 1)
    out[...] = product
    width = product.shape[0]
    both = jnp.concatenate([dot_nt(product, known[...]), dot_nt(product, product)], 1) * scale
    lanes = inner.shape[1]
    for n in range(0, both.shape[1], lanes):
        piece = both[:, n : n + lanes]
        row = n // lanes * width
        inner[row : row + width, : piece.shape[1]] = piece
        if piece.shape[1] < lanes:
            inner[row : row + width, piece.shape[1] :] = jnp.zeros(
                (width, lanes - piece.shape[1]), jnp.float32
            )


def apply_tiles(store, prepared, parts, known, scale):
    near, near_rows, far, far_rows, totals = prepared
    own, above, low, high, below = parts
    block_rows, _, size, _ = store.shape
    width = own.shape[2]
    vmem, smem = pl.BlockSpec(memory_space=pltpu.VMEM), pl.BlockSpec(memory_space=pltpu.SMEM)
    anywhere = pl.BlockSpec(memory_space=pl.ANY)
    total = jax.ShapeDtypeStruct((block_rows, width, size), jnp.float32)

    def scratch(*parts):
        held = sum(p.shape[0] for p in parts) + 1
        return [
            pltpu.VMEM((held,) + own.shape[1:], own.dtype),
            pltpu.SemaphoreType.DMA((len(parts),)),
        ]

    params = pltpu.CompilerParams(vmem_limit_bytes=20 << 20)
    start = pl.pallas_call(
        near_kernel,
        out_shape=total,
        in_specs=[smem] * 3 + [anywhere] * 3 + [vmem],
        out_specs=vmem,
        scratch_shapes=scratch(own, above, below),
        compiler_params=params,
        cost_estimate=pl.CostEstimate(
            flops=1 << 29, bytes_accessed=10 << 20, transcendentals=0
        ),
        name="near_tiles",
    )(near, near_rows, totals, own, above, below, store)
    pieces = -(-(known.shape[0] + width) // size)
    return pl.pallas_call(
        functools.partial(far_kernel, scale),
        out_shape=(
            jax.ShapeDtypeStruct((width, block_rows * size), jnp.float32),
            jax.ShapeDtypeStruct((pieces * width, size), jnp.float32),
        ),
        in_specs=[smem] * 3 + [anywhere] * 2 + [vmem] * 3,
        out_specs=(vmem, vmem),
        scratch_shapes=scratch(low, high) + [pltpu.VMEM(total.shape, total.dtype)],
        compiler_params=params,
        name="far_tiles",
    )(far, far_rows, totals, low, high, store, start, known)


def factor(gram):
    n = gram.shape[0]
    across = 2 * n
    row_ids = lax.broadcasted_iota(jnp.int32, (n, n), 0)
    col_ids = lax.broadcasted_iota(jnp.int32, (n, n), 1)
    eye = jnp.where(row_ids == col_ids, 1.0, 0.0).astype(jnp.float32)
    wide = jnp.concatenate([gram, eye], 1)
    parts = [wide[i : i + SUB] for i in range(0, n, SUB)]
    sub = lax.broadcasted_iota(jnp.int32, (SUB, across), 0)

    def lane(a, k):
        return jnp.broadcast_to(a[:, k : k + 1], (SUB, across))

    for k in range(0, n, 2):
        home, at = divmod(k, SUB)
        one = jnp.broadcast_to(parts[home][at : at + 1], (SUB, across))
        two = jnp.broadcast_to(parts[home][at + 1 : at + 2], (SUB, across))
        head, beside = lane(one, k), lane(one, k + 1)
        head_inv = 1.0 / head
        link = lane(two, k) * head_inv
        tail_inv = 1.0 / (lane(two, k + 1) - link * beside)
        two = two - link * one
        for i in range(home, len(parts)):
            first = lane(parts[i], k) * head_inv
            second = (lane(parts[i], k + 1) - first * beside) * tail_inv
            if i == home:
                first = jnp.where(sub > at, first, 0.0)
                second = jnp.where(sub > at + 1, second, 0.0)
            parts[i] = parts[i] - first * one - second * two
    wide = jnp.concatenate(parts, 0)
    upper = wide[:, :n]
    diag = jnp.sum(jnp.where(row_ids == col_ids, upper, 0.0), 1, keepdims=True)
    scale = lax.rsqrt(diag)
    upper = jnp.where(row_ids <= col_ids, upper * scale, 0.0)
    lower = jnp.where(row_ids >= col_ids, wide[:, n:] * scale, 0.0)
    return upper, lower


def block_of(ref, i, b):
    return ref[i // 2 * b : (i // 2 + 1) * b, i % 2 * b : (i % 2 + 1) * b]


def known_inner(sums, prev, b):
    table, n = {}, 0
    for i in range(prev):
        for j in range(i, prev):
            table[i, j] = block_of(sums, n, b)
            n += 1
    rows = []
    for i in range(prev):
        row = [table[i, j] if i <= j else table[j, i].T for j in range(prev)]
        rows.append(jnp.concatenate(row, 1))
    return jnp.concatenate(rows, 0)


def first_kernel(sums, product, known, fresh, half, upper, cross):
    b = product.shape[0]
    prev = known.shape[0] // b
    count = prev * (prev + 1) // 2
    own = known_inner(sums, prev, b)
    proj = jnp.concatenate([block_of(sums, count + i, b) for i in range(prev)], 1)
    spread = dot_nn(proj, own)
    gram = block_of(sums, count + prev, b) + dot_nt(spread - 2.0 * proj, proj)
    residual = product[...] - dot_nn(proj, known[...])
    up, inverse = factor(gram)
    new = dot_nn(inverse, residual)
    fresh[...] = new
    upper[...] = up
    cross[...] = dot_nn(inverse, proj - spread)
    size = half.shape[2]
    for i in range(half.shape[0]):
        half[i] = new[:, i * size : (i + 1) * size].astype(half.dtype)


def last_kernel(sums, later, cross, product, known, fresh, first_upper, out, uppers):
    b = product.shape[0]
    prev = known.shape[0] // b
    own = known_inner(sums, prev, b)
    old = jnp.concatenate([block_of(later, i, b) for i in range(prev)], 1)
    new = block_of(later, prev, b)
    spread = dot_nn(old, own) + dot_nn(new, cross[...])
    spread_new = dot_nt(old, cross[...]) + new
    gram = (
        block_of(later, prev + 1, b)
        + dot_nt(spread - 2.0 * old, old)
        + dot_nt(spread_new - 2.0 * new, new)
    )
    residual = product[...] - dot_nn(old, known[...]) - dot_nn(new, fresh[...])
    up, inverse = factor(gram)
    out[0] = fresh[...]
    out[1] = dot_nn(inverse, residual)
    uppers[0] = first_upper[...]
    uppers[1] = up


def on_device(tiles, block_columns, live_counts, earlier):
    block_rows, slots, size, _ = tiles.shape
    prev, b, rows_here = earlier.shape
    scale = 1.0 / (rows_here * lax.axis_size("row") * lax.axis_size("col"))
    counts = live_counts.reshape(block_rows)
    here_y = lax.axis_index("col") // NZ
    owner = block_columns // block_rows
    turn = (owner // NZ - here_y) % NY
    picks = (turn * NZ + owner % NZ) * block_rows + block_columns % block_rows
    picks = picks.reshape(-1)
    vmem = pl.BlockSpec(memory_space=pltpu.VMEM)
    f32 = jnp.float32
    known = earlier.reshape(prev * b, rows_here)
    prepared = prepare(tiles, picks, counts)

    def split(a):
        return jnp.transpose(a.reshape(b, block_rows, size), (1, 0, 2))

    parts = gather_group(split(earlier[-1].astype(jnp.bfloat16)))
    inner = jnp.dot(known, known.T, precision=HI) * scale
    blocks = [
        inner[i * b : (i + 1) * b, j * b : (j + 1) * b]
        for i in range(prev)
        for j in range(i, prev)
    ]
    old = [jnp.concatenate(blocks[i : i + 2], 1) for i in range(0, len(blocks), 2)]
    product, mixed = apply_tiles(tiles, prepared, parts, known, scale)
    sums = sum_everywhere(jnp.concatenate(old + [mixed], 0))
    fresh, half, upper, cross = pl.pallas_call(
        first_kernel,
        out_shape=(
            jax.ShapeDtypeStruct((b, rows_here), f32),
            jax.ShapeDtypeStruct((block_rows, b, size), jnp.bfloat16),
            jax.ShapeDtypeStruct((b, b), f32),
            jax.ShapeDtypeStruct((b, prev * b), f32),
        ),
        in_specs=[vmem] * 3,
        out_specs=(vmem,) * 4,
        compiler_params=pltpu.CompilerParams(vmem_limit_bytes=20 << 20),
        name="first_step",
    )(sums, product, known)

    parts = gather_group(half)
    basis = jnp.concatenate([known, fresh], 0)
    product, mixed = apply_tiles(tiles, prepared, parts, basis, scale)
    mixed = jnp.concatenate([mixed, jnp.zeros((256 - mixed.shape[0], size), f32)], 0)
    later = sum_everywhere(mixed)
    return pl.pallas_call(
        last_kernel,
        out_shape=(
            jax.ShapeDtypeStruct((STEPS, b, rows_here), f32),
            jax.ShapeDtypeStruct((STEPS, b, b), f32),
        ),
        in_specs=[vmem] * 7,
        out_specs=(vmem, vmem),
        compiler_params=pltpu.CompilerParams(vmem_limit_bytes=20 << 20),
        name="last_step",
    )(sums, later, cross, product, known, fresh, upper)


def solution(mesh):
    return jax.shard_map(
        on_device,
        mesh=mesh,
        in_specs=(
            P(("row", "col"), None, None, None),
            P(("row", "col"), None),
            P("row", "col"),
            P(None, None, ("row", "col")),
        ),
        out_specs=(P(None, None, ("row", "col")), P()),
        check_vma=False,
    )
```

time: 865 us -> 190 us (0.22)
  waiting for transfers between devices: 636 us -> 32 us
  blocking collectives: 151 us -> 98.6 us
  other arithmetic: 26.4 us -> 0.99 us
  Pallas kernels: 0 us -> 23.1 us
  starting transfers between devices: 0.16 us -> 20 us
  matrix products: 19.7 us -> 1.93 us
  between operations: 13.9 us -> 0.92 us
    psum x2 -> x0, waiting for transfers between devices: 497 us -> none  [on_device(): projections = lax.psum(local_proj, ('row', 'col'))]
    psum x2 -> x0, blocking collectives: 151 us -> none  [on_device(): gram_sum = lax.psum(local_gram, ('row', 'col'))]
    all_gather x2 -> x0, waiting for transfers between devices: 138 us -> none  [the longest x1 71.6 us: on_device(): group_half = lax.all_gather(first_half, 'col', axis=1, tiled=True)]
    all_to_all x0 -> x7, blocking collectives: none -> 98.6 us  [the longest x5 72.8 us: to_all(): lax.all_to_all(copies, axis, 0, 0, axis_index_groups=groups, tiled=True)]
    another operation x12 -> x0, other arithmetic: 24.9 us -> none  [the longest x6 13 us: on_device(): factor_low = jnp.linalg.cholesky(gram_sum)]
    pallas_call x0 -> x7, Pallas kernels: none -> 23.1 us  [the longest x1 6.77 us: on_device(): pl.pallas_call(last_kernel, out_shape=(jax.ShapeDtypeStruct((STEPS, b, ro...]
    dot_general x8 -> x1, matrix products: 18.4 us -> 1.93 us  [on_device(): inner = jnp.dot(known, known.T, precision=HI) * scale]
    ppermute x0 -> x8, waiting for transfers between devices: none -> 16 us  [the longest x2 16 us: gather_group(): below = lax.ppermute(own, 'col', Y_UP)]
  transfers between devices with their start and end apart: 4 -> 9, of which waited for: 4 -> 3; matrix products, arithmetic and copies ran while one was open for 1% -> 2% of each run, Pallas kernels for 0% -> 3%
where the time goes in v2:
time: 190 us; the launch traced here: 189 us
  blocking collectives  98.6 us (52%)
  waiting for transfers between devices  32 us (17%)
  Pallas kernels  23.1 us (12%)
  starting transfers between devices  20 us (11%)
  local copies, waits for them, and re-layouts  11.3 us (6%)
  matrix products  1.93 us (1%)
    all_to_all x5, blocking collectives, to_all(): lax.all_to_all(copies, axis, 0, 0, axis_index_groups=groups, tiled=True)  72.8 us
    all_to_all x2, blocking collectives, sum_everywhere(): lax.all_to_all(part, ALL, 0, 0, axis_index_groups=XY_GROUPS, tiled=True)  25.8 us
    ppermute x2, waiting for transfers between devices, gather_group(): below = lax.ppermute(own, 'col', Y_UP)  16 us
    all_to_all x1, waiting for transfers between devices, to_all(): lax.all_to_all(copies, axis, 0, 0, axis_index_groups=groups, tiled=True)  16 us
    all_to_all x1, starting transfers between devices, to_all(): lax.all_to_all(copies, axis, 0, 0, axis_index_groups=groups, tiled=True)  9 us
    unnamed x13, local copies, waits for them, and re-layouts  8.96 us
    pallas_call x1, Pallas kernels, on_device(): pl.pallas_call(last_kernel, out_shape=(jax.ShapeDtypeStruct((STEPS, b, ro...  6.77 us
    pallas_call x1, Pallas kernels, on_device(): pl.pallas_call(first_kernel, out_shape=(jax.ShapeDtypeStruct((b, rows_her...  5.69 us
  transfers between devices with their start and end apart: 9, of which 3 were waited for; matrix products, arithmetic and copies ran while one was open for 2% of the time, Pallas kernels for 3%

profile of v2, /device:TPU:1, one launch (start us, length us, event | category | flops | bytes accessed | tf_op | source)
XLA Modules:
  0.0 189.0 jit_solution(13077422624544746270)
XLA Ops:
  2.6 9.0 %all-to-all-start = ((bf16[8,4,64,128]{3,2,1,0:T(8,128)(2,1)}), bf16[8,4,64,128]{3,2,1,0:T(8,128)(2,1)S(1)}, u32[]{:S(2)}, u32[]{:S(2)}) async-start(bf16[8,4,64,128]{3,2,1,0:T(8,128)(2,1)} %broadcast_in_dim.12), calls=%async_computation | async-start | bytes 1048576 | tf_op jit(solution)/shard_map/all_to_all | solution.py:48
  11.6 1.9 %convolution_multiply_fusion = f32[256,256]{1,0:T(8,128)S(1)} fusion(f32[256,512]{1,0:T(8,128)} %bitcast.11), kind=kOutput, calls=%fused_computation | convolution fusion | flops 402718720 | bytes 786432 | tf_op jit(solution)/shard_map/dot_general | solution.py:359
  13.6 16.0 %all-to-all-done.own = bf16[8,4,64,128]{3,2,1,0:T(8,128)(2,1)S(1)} async-done(((bf16[8,4,64,128]{3,2,1,0:T(8,128)(2,1)}), bf16[8,4,64,128]{3,2,1,0:T(8,128)(2,1)S(1)}, u32[]{:S(2)}, u32[]{:S(2)}) %all-to-all-start) | async-done | bytes 524320 | tf_op jit(solution)/shard_map/all_to_all | solution.py:48
  33.7 2.3 %prepare.1 = (s32[304]{0:T(512)S(1)}, s32[76]{0:T(128)S(1)}, s32[304]{0:T(512)S(1)}, s32[76]{0:T(128)S(1)}, s32[2]{0:T(128)S(1)}) custom-call(s32[256]{0:T(256)S(1)} %reshape.35.picks, s32[4]{0:T(128)S(1)} %bitcast.19), custom_call_target="tpu_custom_call" | custom-call | bytes 8388608 | tf_op jit(solution)/shard_map/prepare/pallas_call | solution.py:125
  36.2 7.7 %collective-permute-done.below = bf16[8,4,64,128]{3,2,1,0:T(8,128)(2,1)S(1)} collective-permute-done((bf16[8,4,64,128]{3,2,1,0:T(8,128)(2,1)S(1)}, bf16[8,4,64,128]{3,2,1,0:T(8,128)(2,1)S(1)}, u32[]{:S(2)}, u32[]{:S(2)}) %collective-permute-start) | collective-permute-done | bytes 524320 | tf_op jit(solution)/shard_map/ppermute | solution.py:53
  44.0 2.7 %collective-permute-start.3 = (bf16[4,4,64,128]{3,2,1,0:T(8,128)(2,1)S(1)}, bf16[4,4,64,128]{3,2,1,0:T(8,128)(2,1)S(1)}, u32[]{:S(2)}, u32[]{:S(2)}) collective-permute-start(bf16[4,4,64,128]{3,2,1,0:T(8,128)(2,1)S(1)} %slice.52), channel_id=1, source_target_pairs={{0,24},{1,25},{2,26},{3,27},{4,28},{5,29},{6,30},{7,31},{8,0},{9,1... | collective-permute-start | bytes 786440 | tf_op jit(solution)/shard_map/ppermute | solution.py:56
  46.9 3.4 %copy-done = bf16[4,64,128,128]{3,2,1,0:T(8,128)(2,1)S(1)} copy-done((bf16[4,64,128,128]{3,2,1,0:T(8,128)(2,1)S(1)}, bf16[4,64,128,128]{3,2,1,0:T(8,128)(2,1)}, u32[]{:S(2)}) %copy-start) | copy-done | bytes 8388632
  50.3 1.9 near_tiles.2.start
  53.7 2.2 %far_tiles.2 = (f32[64,512]{1,0:T(8,128)S(1)}, f32[192,128]{1,0:T(8,128)S(1)}) custom-call(s32[304]{0:T(512)S(1)} %get-tuple-element.15.table, s32[76]{0:T(128)S(1)} %get-tuple-element.16.rows, s32[2]{0:T(128)S(1)} %get-tuple-element.17.totals, bf16[4,4,64,128]{3,2,1,0:T(8,128)(2,1)S(1)} %collective-permute-done.1.low, ...), custom_call_target="tpu_custom_call" | custom-call | tf_op jit(solution)/shard_map/far_tiles/pallas_call | solution.py:231
  55.9 12.9 %all_to_all.40 = f32[16,32,128]{2,1,0:T(8,128)S(1)} all-to-all(f32[16,32,128]{2,1,0:T(8,128)S(1)} %bitcast.21), channel_id=1, replica_groups={{0,8,16,24,64,72,80,88,128,136,144,152,192,200,208,216},{1,9,17,25,65,7..., dimensions={0} | all-to-all | bytes 524288 | tf_op jit(solution)/shard_map/all_to_all | solution.py:63
  68.8 16.3 %all_to_all.41 = f32[16,32,128]{2,1,0:T(8,128)S(1)} all-to-all(f32[16,32,128]{2,1,0:T(8,128)S(1)} %broadcast_in_dim.13), channel_id=1, replica_groups={{0,1,2,3,4,5,6,7,32,33,34,35,36,37,38,39},{8,9,10,11,12,13,14,15,40,41,..., dimensions={0} | all-to-all | bytes 524288 | tf_op jit(solution)/shard_map/all_to_all | solution.py:48
  85.2 10.5 %all_to_all.42 = f32[16,32,128]{2,1,0:T(8,128)S(1)} all-to-all(f32[16,32,128]{2,1,0:T(8,128)S(1)} %broadcast_in_dim.14), channel_id=1, replica_groups={{0,8,16,24,64,72,80,88,128,136,144,152,192,200,208,216},{1,9,17,25,65,7..., dimensions={0} | all-to-all | bytes 524288 | tf_op jit(solution)/shard_map/all_to_all | solution.py:48
  95.7 5.7 %first_step.1 = (f32[64,512]{1,0:T(8,128)S(1)}, bf16[4,64,128]{2,1,0:T(8,128)(2,1)S(1)}, f32[64,64]{1,0:T(8,128)S(1)}, f32[64,256]{1,0:T(8,128)S(1)}) custom-call(f32[512,128]{1,0:T(8,128)S(1)} %bitcast.16, f32[64,512]{1,0:T(8,128)S(1)} %get-tuple-element.21.product, f32[256,512]{1,0:T(8,128)S(1)} %bitcast.13), custom_call_target="tpu_custom_call" | custom-call | tf_op jit(solution)/shard_map/first_step/pallas_call | solution.py:368
  101.5 19.2 %all_to_all.43.own = bf16[8,4,64,128]{3,2,1,0:T(8,128)(2,1)S(1)} all-to-all(bf16[8,4,64,128]{3,2,1,0:T(8,128)(2,1)S(1)} %broadcast_in_dim.15), channel_id=1, replica_groups={{0,1,2,3,4,5,6,7},{8,9,10,11,12,13,14,15},{16,17,18,19,20,21,22,23},{24..., dimensions={0} | all-to-all | bytes 1048576 | tf_op jit(solution)/shard_map/all_to_all | solution.py:48
  120.9 2.4 %collective-permute-start.6 = (bf16[8,4,64,128]{3,2,1,0:T(8,128)(2,1)S(1)}, bf16[8,4,64,128]{3,2,1,0:T(8,128)(2,1)S(1)}, u32[]{:S(2)}, u32[]{:S(2)}) collective-permute-start(bf16[8,4,64,128]{3,2,1,0:T(8,128)(2,1)S(1)} %all_to_all.43.own), channel_id=1, source_target_pairs={{0,24},{1,25},{2,26},{3,27},{4,28},{5,29},{6,30},{7,31},{8,0},{9,1... | collective-permute-start | bytes 1572872 | tf_op jit(solution)/shard_map/ppermute | solution.py:54
  123.4 8.3 %collective-permute-done.4.below = bf16[8,4,64,128]{3,2,1,0:T(8,128)(2,1)S(1)} collective-permute-done((bf16[8,4,64,128]{3,2,1,0:T(8,128)(2,1)S(1)}, bf16[8,4,64,128]{3,2,1,0:T(8,128)(2,1)S(1)}, u32[]{:S(2)}, u32[]{:S(2)}) %collective-permute-start.4) | collective-permute-done | bytes 524320 | tf_op jit(solution)/shard_map/ppermute | solution.py:53
  131.8 2.7 %collective-permute-start.7 = (bf16[4,4,64,128]{3,2,1,0:T(8,128)(2,1)S(1)}, bf16[4,4,64,128]{3,2,1,0:T(8,128)(2,1)S(1)}, u32[]{:S(2)}, u32[]{:S(2)}) collective-permute-start(bf16[4,4,64,128]{3,2,1,0:T(8,128)(2,1)S(1)} %slice.54), channel_id=1, source_target_pairs={{0,24},{1,25},{2,26},{3,27},{4,28},{5,29},{6,30},{7,31},{8,0},{9,1... | collective-permute-start | bytes 786440 | tf_op jit(solution)/shard_map/ppermute | solution.py:56
  134.6 3.4 %copy-done.2 = bf16[4,64,128,128]{3,2,1,0:T(8,128)(2,1)S(1)} copy-done((bf16[4,64,128,128]{3,2,1,0:T(8,128)(2,1)S(1)}, bf16[4,64,128,128]{3,2,1,0:T(8,128)(2,1)}, u32[]{:S(2)}) %copy-start.2) | copy-done | bytes 8388632
  138.0 2.1 %near_tiles.3.start = f32[4,64,128]{2,1,0:T(8,128)S(1)} custom-call(s32[304]{0:T(512)S(1)} %get-tuple-element.18.table, s32[76]{0:T(128)S(1)} %get-tuple-element.19.rows, s32[2]{0:T(128)S(1)} %get-tuple-element.17.totals, bf16[8,4,64,128]{3,2,1,0:T(8,128)(2,1)S(1)} %all_to_all.43.own, bf16[8,4,64,128]{3,2,1,0:T(8,128)(2,1)S(1)} %collective-permute-done.6.above, ...), custom_call_target="tpu_custom_call" | custom-call | flops 536870912 | bytes 10485760 | tf_op jit(solution)/shard_map/near_tiles/pallas_call | solution.py:218
  140.1 2.3 %far_tiles.3 = (f32[64,512]{1,0:T(8,128)S(1)}, f32[192,128]{1,0:T(8,128)S(1)}) custom-call(s32[304]{0:T(512)S(1)} %get-tuple-element.15.table, s32[76]{0:T(128)S(1)} %get-tuple-element.16.rows, s32[2]{0:T(128)S(1)} %get-tuple-element.17.totals, bf16[4,4,64,128]{3,2,1,0:T(8,128)(2,1)S(1)} %collective-permute-done.5.low, ...), custom_call_target="tpu_custom_call" | custom-call | tf_op jit(solution)/shard_map/far_tiles/pallas_call | solution.py:231
  142.4 12.9 %all_to_all.44 = f32[16,16,128]{2,1,0:T(8,128)S(1)} all-to-all(f32[16,16,128]{2,1,0:T(8,128)S(1)} %bitcast.20), channel_id=1, replica_groups={{0,8,16,24,64,72,80,88,128,136,144,152,192,200,208,216},{1,9,17,25,65,7..., dimensions={0} | all-to-all | bytes 262144 | tf_op jit(solution)/shard_map/all_to_all | solution.py:63
  155.3 17.0 %all_to_all.45 = f32[16,16,128]{2,1,0:T(8,128)S(1)} all-to-all(f32[16,16,128]{2,1,0:T(8,128)S(1)} %broadcast_in_dim.16), channel_id=1, replica_groups={{0,1,2,3,4,5,6,7,32,33,34,35,36,37,38,39},{8,9,10,11,12,13,14,15,40,41,..., dimensions={0} | all-to-all | bytes 262144 | tf_op jit(solution)/shard_map/all_to_all | solution.py:48
  172.4 9.8 %all_to_all.46 = f32[16,16,128]{2,1,0:T(8,128)S(1)} all-to-all(f32[16,16,128]{2,1,0:T(8,128)S(1)} %broadcast_in_dim.17), channel_id=1, replica_groups={{0,8,16,24,64,72,80,88,128,136,144,152,192,200,208,216},{1,9,17,25,65,7..., dimensions={0} | all-to-all | bytes 262144 | tf_op jit(solution)/shard_map/all_to_all | solution.py:48
  182.2 6.8 %last_step.1 = (f32[2,64,512]{2,1,0:T(8,128)}, f32[2,64,64]{2,1,0:T(8,128)}) custom-call(f32[512,128]{1,0:T(8,128)S(1)} %bitcast.17, f32[256,128]{1,0:T(8,128)S(1)} %bitcast.18, f32[64,256]{1,0:T(8,128)S(1)} %get-tuple-element.25.cross, f32[64,512]{1,0:T(8,128)S(1)} %get-tuple-element.26.product, f32[256,512]{1,0:T(8,128)S(1)} %bitcast.15, ...), custom_call_target="tpu_custom_call" | custom-call | tf_op jit(solution)/shard_map/last_step/pallas_call | solution.py:387
  (47 shorter events, 8.7 us)
Async XLA Ops:
  0.6 51.6 %copy-start.3 = (f32[4,64,512]{2,1,0:T(8,128)S(1)}, f32[4,64,512]{2,1,0:T(8,128)}, u32[]{:S(2)}) copy-start(f32[4,64,512]{2,1,0:T(8,128)} %param.7) | copy-start | bytes 1572868
  2.6 27.0 %all-to-all-start = ((bf16[8,4,64,128]{3,2,1,0:T(8,128)(2,1)}), bf16[8,4,64,128]{3,2,1,0:T(8,128)(2,1)S(1)}, u32[]{:S(2)}, u32[]{:S(2)}) async-start(bf16[8,4,64,128]{3,2,1,0:T(8,128)(2,1)} %broadcast_in_dim.12), calls=%async_computation | async-start | bytes 1048576 | tf_op jit(solution)/shard_map/all_to_all | solution.py:48
  29.6 14.3 %collective-permute-start = (bf16[8,4,64,128]{3,2,1,0:T(8,128)(2,1)S(1)}, bf16[8,4,64,128]{3,2,1,0:T(8,128)(2,1)S(1)}, u32[]{:S(2)}, u32[]{:S(2)}) collective-permute-start(bf16[8,4,64,128]{3,2,1,0:T(8,128)(2,1)S(1)} %all-to-all-done.own), channel_id=1, source_target_pairs={{0,8},{1,9},{2,10},{3,11},{4,12},{5,13},{6,14},{7,15},{8,16},{9,17... | collective-permute-start | bytes 1572872 | tf_op jit(solution)/shard_map/ppermute | solution.py:53
  30.8 13.1 %collective-permute-start.2 = (bf16[8,4,64,128]{3,2,1,0:T(8,128)(2,1)S(1)}, bf16[8,4,64,128]{3,2,1,0:T(8,128)(2,1)S(1)}, u32[]{:S(2)}, u32[]{:S(2)}) collective-permute-start(bf16[8,4,64,128]{3,2,1,0:T(8,128)(2,1)S(1)} %all-to-all-done.own), channel_id=1, source_target_pairs={{0,24},{1,25},{2,26},{3,27},{4,28},{5,29},{6,30},{7,31},{8,0},{9,1... | collective-permute-start | bytes 1572872 | tf_op jit(solution)/shard_map/ppermute | solution.py:54
  33.1 0.7 copy-start.4
  43.9 8.3 %collective-permute-start.1 = (bf16[4,4,64,128]{3,2,1,0:T(8,128)(2,1)S(1)}, bf16[4,4,64,128]{3,2,1,0:T(8,128)(2,1)S(1)}, u32[]{:S(2)}, u32[]{:S(2)}) collective-permute-start(bf16[4,4,64,128]{3,2,1,0:T(8,128)(2,1)S(1)} %slice.51), channel_id=1, source_target_pairs={{0,8},{1,9},{2,10},{3,11},{4,12},{5,13},{6,14},{7,15},{8,16},{9,17... | collective-permute-start | bytes 786440 | tf_op jit(solution)/shard_map/ppermute | solution.py:55
  44.0 8.2 %collective-permute-start.3 = (bf16[4,4,64,128]{3,2,1,0:T(8,128)(2,1)S(1)}, bf16[4,4,64,128]{3,2,1,0:T(8,128)(2,1)S(1)}, u32[]{:S(2)}, u32[]{:S(2)}) collective-permute-start(bf16[4,4,64,128]{3,2,1,0:T(8,128)(2,1)S(1)} %slice.52), channel_id=1, source_target_pairs={{0,24},{1,25},{2,26},{3,27},{4,28},{5,29},{6,30},{7,31},{8,0},{9,1... | collective-permute-start | bytes 786440 | tf_op jit(solution)/shard_map/ppermute | solution.py:56
  46.9 3.4 %copy-start = (bf16[4,64,128,128]{3,2,1,0:T(8,128)(2,1)S(1)}, bf16[4,64,128,128]{3,2,1,0:T(8,128)(2,1)}, u32[]{:S(2)}) copy-start(bf16[4,64,128,128]{3,2,1,0:T(8,128)(2,1)} %store.7) | copy-start | bytes 25165828
  50.3 3.4 %copy-start.1 = (bf16[4,64,128,128]{3,2,1,0:T(8,128)(2,1)S(1)}, bf16[4,64,128,128]{3,2,1,0:T(8,128)(2,1)}, u32[]{:S(2)}) copy-start(bf16[4,64,128,128]{3,2,1,0:T(8,128)(2,1)} %store.7) | copy-start | bytes 25165828
  120.7 11.0 %collective-permute-start.4 = (bf16[8,4,64,128]{3,2,1,0:T(8,128)(2,1)S(1)}, bf16[8,4,64,128]{3,2,1,0:T(8,128)(2,1)S(1)}, u32[]{:S(2)}, u32[]{:S(2)}) collective-permute-start(bf16[8,4,64,128]{3,2,1,0:T(8,128)(2,1)S(1)} %all_to_all.43.own), channel_id=1, source_target_pairs={{0,8},{1,9},{2,10},{3,11},{4,12},{5,13},{6,14},{7,15},{8,16},{9,17... | collective-permute-start | bytes 1572872 | tf_op jit(solution)/shard_map/ppermute | solution.py:53
  120.9 10.9 %collective-permute-start.6 = (bf16[8,4,64,128]{3,2,1,0:T(8,128)(2,1)S(1)}, bf16[8,4,64,128]{3,2,1,0:T(8,128)(2,1)S(1)}, u32[]{:S(2)}, u32[]{:S(2)}) collective-permute-start(bf16[8,4,64,128]{3,2,1,0:T(8,128)(2,1)S(1)} %all_to_all.43.own), channel_id=1, source_target_pairs={{0,24},{1,25},{2,26},{3,27},{4,28},{5,29},{6,30},{7,31},{8,0},{9,1... | collective-permute-start | bytes 1572872 | tf_op jit(solution)/shard_map/ppermute | solution.py:54
  131.7 8.4 %collective-permute-start.5 = (bf16[4,4,64,128]{3,2,1,0:T(8,128)(2,1)S(1)}, bf16[4,4,64,128]{3,2,1,0:T(8,128)(2,1)S(1)}, u32[]{:S(2)}, u32[]{:S(2)}) collective-permute-start(bf16[4,4,64,128]{3,2,1,0:T(8,128)(2,1)S(1)} %slice.53), channel_id=1, source_target_pairs={{0,8},{1,9},{2,10},{3,11},{4,12},{5,13},{6,14},{7,15},{8,16},{9,17... | collective-permute-start | bytes 786440 | tf_op jit(solution)/shard_map/ppermute | solution.py:55
  131.8 8.3 %collective-permute-start.7 = (bf16[4,4,64,128]{3,2,1,0:T(8,128)(2,1)S(1)}, bf16[4,4,64,128]{3,2,1,0:T(8,128)(2,1)S(1)}, u32[]{:S(2)}, u32[]{:S(2)}) collective-permute-start(bf16[4,4,64,128]{3,2,1,0:T(8,128)(2,1)S(1)} %slice.54), channel_id=1, source_target_pairs={{0,24},{1,25},{2,26},{3,27},{4,28},{5,29},{6,30},{7,31},{8,0},{9,1... | collective-permute-start | bytes 786440 | tf_op jit(solution)/shard_map/ppermute | solution.py:56
  134.6 3.4 %copy-start.2 = (bf16[4,64,128,128]{3,2,1,0:T(8,128)(2,1)S(1)}, bf16[4,64,128,128]{3,2,1,0:T(8,128)(2,1)}, u32[]{:S(2)}) copy-start(bf16[4,64,128,128]{3,2,1,0:T(8,128)(2,1)} %store.7) | copy-start | bytes 25165828

commit v3 on v2

--- a/solution.py
+++ b/solution.py
@@ -10,12 +10,12 @@
 STEPS = 2
 NX, NY, NZ, NC = 4, 4, 8, 2
 SUB = 8
-GROUP = 4
-AT_ONCE = 4
-FAR = 2
-VECTORS = 32
-CODE = 128
-DEAD = CODE - 1
+PIVOTS = 4
+GROUP, GROUP_BITS = 4, 2
+AT_ONCE, TRIP_BITS = 8, 5
+VECTORS, VECTOR_BITS = 32, 5
+DEAD = (VECTORS, 2 * VECTORS, VECTORS)
+CODE, CODE_BITS = 128, 7
 HI = lax.Precision.HIGHEST
 
 
@@ -48,13 +48,15 @@
     return lax.all_to_all(copies, axis, 0, 0, axis_index_groups=groups, tiled=True)
 
 
-def gather_group(half):
-    own = to_all(half, "col", NZ, Z_GROUPS)
-    below = lax.ppermute(own, "col", Y_UP)
-    above = lax.ppermute(own, "col", Y_DOWN)
-    far_low = lax.ppermute(below[: NZ // 2], "col", Y_UP)
-    far_high = lax.ppermute(above[NZ // 2 :], "col", Y_DOWN)
-    return own, above, far_low, far_high, below
+def gather_beside(own):
+    first, last = own[: NZ // 2], own[NZ // 2 :]
+    onward = lax.ppermute(first, "col", Y_UP), lax.ppermute(last, "col", Y_DOWN)
+    rest = lax.ppermute(last, "col", Y_UP), lax.ppermute(first, "col", Y_DOWN)
+    return onward, rest
+
+
+def gather_beyond(onward):
+    return lax.ppermute(onward[0], "col", Y_UP), lax.ppermute(onward[1], "col", Y_DOWN)
 
 
 def sum_everywhere(a):
@@ -78,65 +80,64 @@
     )
 
 
-def prepare_kernel(slots, picks, counts, near, near_rows, far, far_rows, totals):
+def prepare_kernel(slots, picks, counts, *refs):
     block_rows = counts.shape[0]
-
-    def sort(r, carry):
-        def one(s, carry):
-            a, f = carry
+    tables, rows, totals = refs[:3], refs[3:6], refs[6]
+
+    def sort(r, ends):
+        def one(s, ends):
             pick = picks[r * slots + s]
-            turn = pick // VECTORS
-            beyond = (turn == FAR).astype(jnp.int32)
-            after = (turn > FAR).astype(jnp.int32)
-            near[a] = s * CODE + pick - after * VECTORS
-            far[f] = s * CODE + pick - FAR * VECTORS
-            return a + 1 - beyond, f + beyond
-
-        def fill(table, rows, start, end):
+            turn = pick >> VECTOR_BITS
+            tile = (r * slots + s) * CODE + (pick & (VECTORS - 1))
+            tables[0][ends[0]] = tile
+            tables[1][ends[1]] = tile + ((turn >> 1) << VECTOR_BITS)
+            tables[2][ends[2]] = tile
+            return (
+                ends[0] + jnp.where(turn == 0, 1, 0),
+                ends[1] + (turn & 1),
+                ends[2] + jnp.where(turn == 2, 1, 0),
+            )
+
+        starts, stops = ends, []
+        ends = lax.fori_loop(0, counts[r], one, ends)
+        for table, row, start, end, dead in zip(tables, rows, starts, ends, DEAD):
             for j in range(GROUP):
-                table[end + j] = DEAD
-            stop = (end + GROUP - 1) // GROUP
-
-            def mark(c, _):
-                rows[c] = r
+                table[end + j] = r * slots * CODE + dead
+            stop = (end + GROUP - 1) >> GROUP_BITS
+
+            def mark(c, _, row=row):
+                row[c] = r
                 return 0
 
-            lax.fori_loop(start // GROUP, stop, mark, 0)
-            return stop * GROUP
-
-        a, f = lax.fori_loop(0, counts[r], one, carry)
-        return fill(near, near_rows, carry[0], a), fill(far, far_rows, carry[1], f)
-
-    a, f = lax.fori_loop(0, block_rows, sort, (jnp.int32(0), jnp.int32(0)))
-    for n, (table, rows, end) in enumerate(((near, near_rows, a), (far, far_rows, f))):
+            lax.fori_loop(start >> GROUP_BITS, stop, mark, 0)
+            stops.append(stop << GROUP_BITS)
+        return tuple(stops)
+
+    ends = lax.fori_loop(0, block_rows, sort, (jnp.int32(0),) * 3)
+    for n, (table, row, end, dead) in enumerate(zip(tables, rows, ends, DEAD)):
         for j in range(GROUP * AT_ONCE):
-            table[end + j] = DEAD
+            table[end + j] = dead
         for j in range(AT_ONCE):
-            rows[end // GROUP + j] = 0
-        totals[n] = (end + GROUP * AT_ONCE - 1) // (GROUP * AT_ONCE)
-
-
-def prepare(tiles, picks, counts):
-    block_rows, slots = tiles.shape[:2]
+            row[(end >> GROUP_BITS) + j] = 0
+        totals[n] = (end + GROUP * AT_ONCE - 1) >> TRIP_BITS
+
+
+def prepare(picks, counts, slots):
+    block_rows = counts.shape[0]
     smem = pl.BlockSpec(memory_space=pltpu.SMEM)
     entries = block_rows * (slots + GROUP) + 2 * GROUP * AT_ONCE
     table = jax.ShapeDtypeStruct((entries,), jnp.int32)
     rows = jax.ShapeDtypeStruct((entries // GROUP,), jnp.int32)
-    return pl.pallas_call(
+    out = pl.pallas_call(
         functools.partial(prepare_kernel, slots),
-        out_shape=(
-            table,
-            rows,
-            table,
-            rows,
-            jax.ShapeDtypeStruct((2,), jnp.int32),
-        ),
+        out_shape=(table,) * 3 + (rows,) * 3 + (jax.ShapeDtypeStruct((3,), jnp.int32),),
         in_specs=[smem, smem],
-        out_specs=(smem,) * 5,
+        out_specs=(smem,) * 7,
         compiler_params=pltpu.CompilerParams(vmem_limit_bytes=16 << 20),
         cost_estimate=pl.CostEstimate(flops=0, bytes_accessed=8 << 20, transcendentals=0),
         name="prepare",
     )(picks, counts)
+    return [(out[n], out[3 + n], out[6]) for n in range(3)]
 
 
 def multiply(table, rows, trips, parts, store, group, sems, total):
@@ -150,20 +151,16 @@
     group[start] = jnp.zeros(group.shape[1:], group.dtype)
     for c in copies:
         c.wait()
-    block_rows = group.shape[1]
-    dead = start * block_rows
 
     def step(t, carry):
         for c in range(AT_ONCE):
             chunk = t * AT_ONCE + c
-            r = rows[chunk]
             left, right = [], []
             for j in range(GROUP):
                 code = table[chunk * GROUP + j]
-                pick = jnp.minimum(code % CODE, dead)
-                left.append(group[pick // block_rows, pick % block_rows])
-                right.append(store[r, code // CODE])
-            total[r] += lax.dot_general(
+                left.append(group[code & (CODE - 1)])
+                right.append(store[code >> CODE_BITS])
+            total[rows[chunk]] += lax.dot_general(
                 jnp.concatenate(left, 1),
                 jnp.concatenate(right, 1),
                 (((1,), (1,)), ((), ())),
@@ -174,15 +171,21 @@
     lax.fori_loop(0, trips, step, 0)
 
 
-def near_kernel(table, rows, totals, own, above, below, store, total, group, sems):
+def own_kernel(table, rows, totals, own, store, total, group, sems):
     total[...] = jnp.zeros_like(total)
-    multiply(table, rows, totals[0], (own, above, below), store, group, sems, total)
+    multiply(table, rows, totals[0], (own,), store, group, sems, total)
+
+
+def side_kernel(table, rows, totals, *refs):
+    parts, (store, start, total, group, sems) = refs[:4], refs[4:]
+    total[...] = start[...]
+    multiply(table, rows, totals[1], parts, store, group, sems, total)
 
 
 def far_kernel(scale, table, rows, totals, low, high, store, start, known, *refs):
     out, inner, group, sems, total = refs
     total[...] = start[...]
-    multiply(table, rows, totals[1], (low, high), store, group, sems, total)
+    multiply(table, rows, totals[2], (low, high), store, group, sems, total)
     product = jnp.concatenate([total[r] for r in range(total.shape[0])], 1)
     out[...] = product
     width = product.shape[0]
@@ -198,35 +201,56 @@
             )
 
 
-def apply_tiles(store, prepared, parts, known, scale):
-    near, near_rows, far, far_rows, totals = prepared
-    own, above, low, high, below = parts
+def apply_tiles(store, prepared, own, known, scale):
     block_rows, _, size, _ = store.shape
+    store = store.reshape(-1, size, size)
     width = own.shape[2]
     vmem, smem = pl.BlockSpec(memory_space=pltpu.VMEM), pl.BlockSpec(memory_space=pltpu.SMEM)
     anywhere = pl.BlockSpec(memory_space=pl.ANY)
     total = jax.ShapeDtypeStruct((block_rows, width, size), jnp.float32)
 
-    def scratch(*parts):
+    def flat(parts):
+        return [p.reshape((-1,) + p.shape[2:]) for p in parts]
+
+    def scratch(parts):
         held = sum(p.shape[0] for p in parts) + 1
         return [
-            pltpu.VMEM((held,) + own.shape[1:], own.dtype),
+            pltpu.VMEM((held,) + parts[0].shape[1:], parts[0].dtype),
             pltpu.SemaphoreType.DMA((len(parts),)),
         ]
 
-    params = pltpu.CompilerParams(vmem_limit_bytes=20 << 20)
+    def shared(mib):
+        return dict(
+            compiler_params=pltpu.CompilerParams(vmem_limit_bytes=16 << 20),
+            cost_estimate=pl.CostEstimate(
+                flops=1 << 28, bytes_accessed=mib << 20, transcendentals=0
+            ),
+        )
+
+    onward, rest = gather_beside(own)
+    parts = flat((own,))
     start = pl.pallas_call(
-        near_kernel,
+        own_kernel,
         out_shape=total,
-        in_specs=[smem] * 3 + [anywhere] * 3 + [vmem],
+        in_specs=[smem] * 3 + [anywhere, vmem],
         out_specs=vmem,
-        scratch_shapes=scratch(own, above, below),
-        compiler_params=params,
-        cost_estimate=pl.CostEstimate(
-            flops=1 << 29, bytes_accessed=10 << 20, transcendentals=0
-        ),
-        name="near_tiles",
-    )(near, near_rows, totals, own, above, below, store)
+        scratch_shapes=scratch(parts),
+        name="own_tiles",
+        **shared(8),
+    )(*prepared[0], *parts, store)
+    onward, start = lax.optimization_barrier((onward, start))
+    beyond = gather_beyond(onward)
+    parts = flat((rest[1], onward[1], onward[0], rest[0]))
+    start = pl.pallas_call(
+        side_kernel,
+        out_shape=total,
+        in_specs=[smem] * 3 + [anywhere] * 4 + [vmem] * 2,
+        out_specs=vmem,
+        scratch_shapes=scratch(parts),
+        name="side_tiles",
+        **shared(10),
+    )(*prepared[1], *parts, store, start)
+    parts = flat(beyond)
     pieces = -(-(known.shape[0] + width) // size)
     return pl.pallas_call(
         functools.partial(far_kernel, scale),
@@ -236,10 +260,10 @@
         ),
         in_specs=[smem] * 3 + [anywhere] * 2 + [vmem] * 3,
         out_specs=(vmem, vmem),
-        scratch_shapes=scratch(low, high) + [pltpu.VMEM(total.shape, total.dtype)],
-        compiler_params=params,
+        scratch_shapes=scratch(parts) + [pltpu.VMEM(total.shape, total.dtype)],
         name="far_tiles",
-    )(far, far_rows, totals, low, high, store, start, known)
+        **shared(8),
+    )(*prepared[2], *parts, store, start, known)
 
 
 def factor(gram):
@@ -255,22 +279,31 @@
     def lane(a, k):
         return jnp.broadcast_to(a[:, k : k + 1], (SUB, across))
 
-    for k in range(0, n, 2):
+    for k in range(0, n, PIVOTS):
         home, at = divmod(k, SUB)
-        one = jnp.broadcast_to(parts[home][at : at + 1], (SUB, across))
-        two = jnp.broadcast_to(parts[home][at + 1 : at + 2], (SUB, across))
-        head, beside = lane(one, k), lane(one, k + 1)
-        head_inv = 1.0 / head
-        link = lane(two, k) * head_inv
-        tail_inv = 1.0 / (lane(two, k + 1) - link * beside)
-        two = two - link * one
+        rows = [
+            jnp.broadcast_to(parts[home][at + i : at + i + 1], (SUB, across))
+            for i in range(PIVOTS)
+        ]
+        head = [[lane(rows[i], k + j) if i <= j else None for j in range(PIVOTS)] for i in range(PIVOTS)]
+        inv = []
+        for i in range(PIVOTS):
+            inv.append(1.0 / head[i][i])
+            for j in range(i + 1, PIVOTS):
+                link = head[i][j] * inv[i]
+                rows[j] = rows[j] - link * rows[i]
+                for m in range(j, PIVOTS):
+                    head[j][m] = head[j][m] - link * head[i][m]
         for i in range(home, len(parts)):
-            first = lane(parts[i], k) * head_inv
-            second = (lane(parts[i], k + 1) - first * beside) * tail_inv
-            if i == home:
-                first = jnp.where(sub > at, first, 0.0)
-                second = jnp.where(sub > at + 1, second, 0.0)
-            parts[i] = parts[i] - first * one - second * two
+            links = []
+            for j in range(PIVOTS):
+                link = lane(parts[i], k + j)
+                for m in range(j):
+                    link = link - links[m] * head[m][j]
+                links.append(link * inv[j])
+            for j in range(PIVOTS):
+                link = jnp.where(sub > at + j, links[j], 0.0) if i == home else links[j]
+                parts[i] = parts[i] - link * rows[j]
     wide = jnp.concatenate(parts, 0)
     upper = wide[:, :n]
     diag = jnp.sum(jnp.where(row_ids == col_ids, upper, 0.0), 1, keepdims=True)
@@ -350,12 +383,13 @@
     vmem = pl.BlockSpec(memory_space=pltpu.VMEM)
     f32 = jnp.float32
     known = earlier.reshape(prev * b, rows_here)
-    prepared = prepare(tiles, picks, counts)
+    prepared = prepare(picks, counts, slots)
 
     def split(a):
         return jnp.transpose(a.reshape(b, block_rows, size), (1, 0, 2))
 
-    parts = gather_group(split(earlier[-1].astype(jnp.bfloat16)))
+    own = to_all(split(earlier[-1].astype(jnp.bfloat16)), "col", NZ, Z_GROUPS)
+    own, prepared = lax.optimization_barrier((own, prepared))
     inner = jnp.dot(known, known.T, precision=HI) * scale
     blocks = [
         inner[i * b : (i + 1) * b, j * b : (j + 1) * b]
@@ -363,7 +397,7 @@
         for j in range(i, prev)
     ]
     old = [jnp.concatenate(blocks[i : i + 2], 1) for i in range(0, len(blocks), 2)]
-    product, mixed = apply_tiles(tiles, prepared, parts, known, scale)
+    product, mixed = apply_tiles(tiles, prepared, own, known, scale)
     sums = sum_everywhere(jnp.concatenate(old + [mixed], 0))
     fresh, half, upper, cross = pl.pallas_call(
         first_kernel,
@@ -379,9 +413,9 @@
         name="first_step",
     )(sums, product, known)
 
-    parts = gather_group(half)
+    own = to_all(half, "col", NZ, Z_GROUPS)
     basis = jnp.concatenate([known, fresh], 0)
-    product, mixed = apply_tiles(tiles, prepared, parts, basis, scale)
+    product, mixed = apply_tiles(tiles, prepared, own, basis, scale)
     mixed = jnp.concatenate([mixed, jnp.zeros((256 - mixed.shape[0], size), f32)], 0)
     later = sum_everywhere(mixed)
     return pl.pallas_call(

time: 190 us -> 179 us (0.942)
  waiting for transfers between devices: 32 us -> 22.2 us
  blocking collectives: 98.6 us -> 92.1 us
  starting transfers between devices: 20 us -> 24.3 us
    all_to_all x2, blocking collectives: 25.8 us -> 20.7 us  [sum_everywhere(): lax.all_to_all(part, ALL, 0, 0, axis_index_groups=XY_GROUPS, tiled=True)]
    all_to_all x1, waiting for transfers between devices: 16 us -> 11 us  [to_all(): lax.all_to_all(copies, axis, 0, 0, axis_index_groups=groups, tiled=True)]
    ppermute x8 -> x12, waiting for transfers between devices: 16 us -> 11.1 us  [the longest x2 7.53 us: gather_beyond(): lax.ppermute(onward[0], 'col', Y_UP)]
    ppermute x8 -> x12, starting transfers between devices: 11 us -> 15.3 us  [the longest x4 5.53 us: gather_beside(): rest = (lax.ppermute(last, 'col', Y_UP), lax.ppermute(first, 'col', Y_DOWN))]
    pallas_call x2 -> x4, Pallas kernels: 3.96 us -> 7.55 us  [the longest x2 4.33 us: apply_tiles(): pl.pallas_call(side_kernel, out_shape=total, in_specs=[smem] * 3 + [anywh...]
  transfers between devices with their start and end apart: 9 -> 13, of which waited for: 3 -> 6; matrix products, arithmetic and copies ran while one was open for 2% -> 2% of each run, Pallas kernels for 3% -> 6%
where the time goes in v3:
time: 179 us; the launch traced here: 177 us
  blocking collectives  92.1 us (51%)
  Pallas kernels  24.8 us (14%)
  starting transfers between devices  24.3 us (14%)
  waiting for transfers between devices  22.2 us (12%)
  local copies, waits for them, and re-layouts  9.79 us (5%)
  matrix products  1.94 us (1%)
    all_to_all x5, blocking collectives, to_all(): lax.all_to_all(copies, axis, 0, 0, axis_index_groups=groups, tiled=True)  71.4 us
    all_to_all x2, blocking collectives, sum_everywhere(): lax.all_to_all(part, ALL, 0, 0, axis_index_groups=XY_GROUPS, tiled=True)  20.7 us
    all_to_all x1, waiting for transfers between devices, to_all(): lax.all_to_all(copies, axis, 0, 0, axis_index_groups=groups, tiled=True)  11 us
    all_to_all x1, starting transfers between devices, to_all(): lax.all_to_all(copies, axis, 0, 0, axis_index_groups=groups, tiled=True)  9 us
    ppermute x2, waiting for transfers between devices, gather_beyond(): lax.ppermute(onward[0], 'col', Y_UP)  7.53 us
    unnamed x13, local copies, waits for them, and re-layouts  7.51 us
    ppermute x4, starting transfers between devices, gather_beside(): rest = (lax.ppermute(last, 'col', Y_UP), lax.ppermute(first, 'col', Y_DOWN))  5.53 us
    ppermute x2, starting transfers between devices, gather_beyond(): lax.ppermute(onward[1], 'col', Y_DOWN)  5.34 us
  transfers between devices with their start and end apart: 13, of which 6 were waited for; matrix products, arithmetic and copies ran while one was open for 2% of the time, Pallas kernels for 6%

profile of v3, /device:TPU:1, one launch (start us, length us, event | category | flops | bytes accessed | tf_op | source)
XLA Modules:
  0.0 177.0 jit_solution(5146923249830116515)
XLA Ops:
  2.5 9.0 %all-to-all-start = ((bf16[8,4,64,128]{3,2,1,0:T(8,128)(2,1)}), bf16[8,4,64,128]{3,2,1,0:T(8,128)(2,1)S(1)}, u32[]{:S(2)}, u32[]{:S(2)}) async-start(bf16[8,4,64,128]{3,2,1,0:T(8,128)(2,1)} %broadcast_in_dim.12), calls=%async_computation | async-start | bytes 1048576 | tf_op jit(solution)/shard_map/all_to_all | solution.py:48
  13.0 3.5 %prepare.1 = (s32[336]{0:T(512)S(1)}, s32[336]{0:T(512)S(1)}, s32[336]{0:T(512)S(1)}, s32[84]{0:T(128)S(1)}, s32[84]{0:T(128)S(1)}, /*index=5*/s32[84]{0:T(128)S(1)}, s32[3]{0:T(128)S(1)}) custom-call(s32[256]{0:T(256)S(1)} %reshape.81.picks, s32[4]{0:T(128)S(1)} %bitcast.52), custom_call_target="tpu_custom_call" | custom-call | bytes 8388608 | tf_op jit(solution)/shard_map/prepare/pallas_call | solution.py:131
  18.4 11.0 %all-to-all-done = bf16[8,4,64,128]{3,2,1,0:T(8,128)(2,1)S(1)} async-done(((bf16[8,4,64,128]{3,2,1,0:T(8,128)(2,1)}), bf16[8,4,64,128]{3,2,1,0:T(8,128)(2,1)S(1)}, u32[]{:S(2)}, u32[]{:S(2)}) %all-to-all-start) | async-done | bytes 524320 | tf_op jit(solution)/shard_map/all_to_all | solution.py:48
  29.5 2.8 %collective-permute-start.1 = (bf16[4,4,64,128]{3,2,1,0:T(8,128)(2,1)S(1)}, bf16[4,4,64,128]{3,2,1,0:T(8,128)(2,1)S(1)}, u32[]{:S(2)}, u32[]{:S(2)}) collective-permute-start(bf16[4,4,64,128]{3,2,1,0:T(8,128)(2,1)S(1)} %get-tuple-element.66), channel_id=1, source_target_pairs={{0,24},{1,25},{2,26},{3,27},{4,28},{5,29},{6,30},{7,31},{8,0},{9,1... | collective-permute-start | bytes 786440 | tf_op jit(solution)/shard_map/ppermute | solution.py:53
  32.5 2.7 %collective-permute-start.4 = (bf16[4,4,64,128]{3,2,1,0:T(8,128)(2,1)S(1)}, bf16[4,4,64,128]{3,2,1,0:T(8,128)(2,1)S(1)}, u32[]{:S(2)}, u32[]{:S(2)}) collective-permute-start(bf16[4,4,64,128]{3,2,1,0:T(8,128)(2,1)S(1)} %get-tuple-element.67), channel_id=1, source_target_pairs={{0,24},{1,25},{2,26},{3,27},{4,28},{5,29},{6,30},{7,31},{8,0},{9,1... | collective-permute-start | bytes 786440 | tf_op jit(solution)/shard_map/ppermute | solution.py:54
  35.3 3.4 %copy-done = bf16[4,64,128,128]{3,2,1,0:T(8,128)(2,1)S(1)} copy-done((bf16[4,64,128,128]{3,2,1,0:T(8,128)(2,1)S(1)}, bf16[4,64,128,128]{3,2,1,0:T(8,128)(2,1)}, u32[]{:S(2)}) %copy-start) | copy-done | bytes 8388632
  40.6 2.7 %collective-permute-start.3 = (bf16[4,4,64,128]{3,2,1,0:T(8,128)(2,1)S(1)}, bf16[4,4,64,128]{3,2,1,0:T(8,128)(2,1)S(1)}, u32[]{:S(2)}, u32[]{:S(2)}) collective-permute-start(bf16[4,4,64,128]{3,2,1,0:T(8,128)(2,1)S(1)} %collective-permute-done.1), channel_id=1, source_target_pairs={{0,24},{1,25},{2,26},{3,27},{4,28},{5,29},{6,30},{7,31},{8,0},{9,1... | collective-permute-start | bytes 786440 | tf_op jit(solution)/shard_map/ppermute | solution.py:59
  43.5 2.7 %collective-permute-done.5 = bf16[4,4,64,128]{3,2,1,0:T(8,128)(2,1)S(1)} collective-permute-done((bf16[4,4,64,128]{3,2,1,0:T(8,128)(2,1)S(1)}, bf16[4,4,64,128]{3,2,1,0:T(8,128)(2,1)S(1)}, u32[]{:S(2)}, u32[]{:S(2)}) %collective-permute-start.5) | collective-permute-done | bytes 262176 | tf_op jit(solution)/shard_map/ppermute | solution.py:54
  48.4 3.4 %collective-permute-done.2 = bf16[4,4,64,128]{3,2,1,0:T(8,128)(2,1)S(1)} collective-permute-done((bf16[4,4,64,128]{3,2,1,0:T(8,128)(2,1)S(1)}, bf16[4,4,64,128]{3,2,1,0:T(8,128)(2,1)S(1)}, u32[]{:S(2)}, u32[]{:S(2)}) %collective-permute-start.2) | collective-permute-done | bytes 262176 | tf_op jit(solution)/shard_map/ppermute | solution.py:59
  51.9 2.4 %far_tiles.2 = (f32[64,512]{1,0:T(8,128)S(1)}, f32[192,128]{1,0:T(8,128)S(1)}) custom-call(s32[336]{0:T(512)S(1)} %get-tuple-element.40.table, s32[84]{0:T(128)S(1)} %get-tuple-element.41.rows, s32[3]{0:T(128)S(1)} %get-tuple-element.51.totals, bf16[16,64,128]{2,1,0:T(8,128)(2,1)S(1)} %bitcast.45, bf16[16,64,128]{2,1,0:T(8,128)(2,1)S(1)} %bitcast.47, ...), custom_call_target="tpu_custom_call" | custom-call | flops 268435456 | bytes 8388608 | tf_op jit(solution)/shard_map/far_tiles/pallas_call | solution.py:255
  54.3 11.2 %all_to_all.40 = f32[16,32,128]{2,1,0:T(8,128)S(1)} all-to-all(f32[16,32,128]{2,1,0:T(8,128)S(1)} %bitcast.54), channel_id=1, replica_groups={{0,8,16,24,64,72,80,88,128,136,144,152,192,200,208,216},{1,9,17,25,65,7..., dimensions={0} | all-to-all | bytes 524288 | tf_op jit(solution)/shard_map/all_to_all | solution.py:65
  65.5 14.9 %all_to_all.41 = f32[16,32,128]{2,1,0:T(8,128)S(1)} all-to-all(f32[16,32,128]{2,1,0:T(8,128)S(1)} %broadcast_in_dim.13), channel_id=1, replica_groups={{0,1,2,3,4,5,6,7,32,33,34,35,36,37,38,39},{8,9,10,11,12,13,14,15,40,41,..., dimensions={0} | all-to-all | bytes 524288 | tf_op jit(solution)/shard_map/all_to_all | solution.py:48
  80.5 10.5 %all_to_all.42 = f32[16,32,128]{2,1,0:T(8,128)S(1)} all-to-all(f32[16,32,128]{2,1,0:T(8,128)S(1)} %broadcast_in_dim.14), channel_id=1, replica_groups={{0,8,16,24,64,72,80,88,128,136,144,152,192,200,208,216},{1,9,17,25,65,7..., dimensions={0} | all-to-all | bytes 524288 | tf_op jit(solution)/shard_map/all_to_all | solution.py:48
  91.0 3.9 %first_step.1 = (f32[64,512]{1,0:T(8,128)S(1)}, bf16[4,64,128]{2,1,0:T(8,128)(2,1)S(1)}, f32[64,64]{1,0:T(8,128)S(1)}, f32[64,256]{1,0:T(8,128)S(1)}) custom-call(f32[512,128]{1,0:T(8,128)S(1)} %bitcast.37, f32[64,512]{1,0:T(8,128)S(1)} %get-tuple-element.54.product, f32[256,512]{1,0:T(8,128)S(1)} %bitcast.32), custom_call_target="tpu_custom_call" | custom-call | tf_op jit(solution)/shard_map/first_step/pallas_call | solution.py:402
  95.1 19.2 %all_to_all.43 = bf16[8,4,64,128]{3,2,1,0:T(8,128)(2,1)S(1)} all-to-all(bf16[8,4,64,128]{3,2,1,0:T(8,128)(2,1)S(1)} %broadcast_in_dim.15), channel_id=1, replica_groups={{0,1,2,3,4,5,6,7},{8,9,10,11,12,13,14,15},{16,17,18,19,20,21,22,23},{24..., dimensions={0} | all-to-all | bytes 1048576 | tf_op jit(solution)/shard_map/all_to_all | solution.py:48
  116.1 2.5 %collective-permute-start.10 = (bf16[4,4,64,128]{3,2,1,0:T(8,128)(2,1)S(1)}, bf16[4,4,64,128]{3,2,1,0:T(8,128)(2,1)S(1)}, u32[]{:S(2)}, u32[]{:S(2)}) collective-permute-start(bf16[4,4,64,128]{3,2,1,0:T(8,128)(2,1)S(1)} %get-tuple-element.65), channel_id=1, source_target_pairs={{0,24},{1,25},{2,26},{3,27},{4,28},{5,29},{6,30},{7,31},{8,0},{9,1... | collective-permute-start | bytes 786440 | tf_op jit(solution)/shard_map/ppermute | solution.py:54
  118.6 3.4 %copy-done.2 = bf16[4,64,128,128]{3,2,1,0:T(8,128)(2,1)S(1)} copy-done((bf16[4,64,128,128]{3,2,1,0:T(8,128)(2,1)S(1)}, bf16[4,64,128,128]{3,2,1,0:T(8,128)(2,1)}, u32[]{:S(2)}) %copy-start.2) | copy-done | bytes 8388632
  123.7 2.7 %collective-permute-start.9 = (bf16[4,4,64,128]{3,2,1,0:T(8,128)(2,1)S(1)}, bf16[4,4,64,128]{3,2,1,0:T(8,128)(2,1)S(1)}, u32[]{:S(2)}, u32[]{:S(2)}) collective-permute-start(bf16[4,4,64,128]{3,2,1,0:T(8,128)(2,1)S(1)} %collective-permute-done.7), channel_id=1, source_target_pairs={{0,24},{1,25},{2,26},{3,27},{4,28},{5,29},{6,30},{7,31},{8,0},{9,1... | collective-permute-start | bytes 786440 | tf_op jit(solution)/shard_map/ppermute | solution.py:59
  129.1 4.1 %collective-permute-done.8 = bf16[4,4,64,128]{3,2,1,0:T(8,128)(2,1)S(1)} collective-permute-done((bf16[4,4,64,128]{3,2,1,0:T(8,128)(2,1)S(1)}, bf16[4,4,64,128]{3,2,1,0:T(8,128)(2,1)S(1)}, u32[]{:S(2)}, u32[]{:S(2)}) %collective-permute-start.8) | collective-permute-done | bytes 262176 | tf_op jit(solution)/shard_map/ppermute | solution.py:59
  133.2 2.5 %far_tiles.3 = (f32[64,512]{1,0:T(8,128)S(1)}, f32[192,128]{1,0:T(8,128)S(1)}) custom-call(s32[336]{0:T(512)S(1)} %get-tuple-element.40.table, s32[84]{0:T(128)S(1)} %get-tuple-element.41.rows, s32[3]{0:T(128)S(1)} %get-tuple-element.51.totals, bf16[16,64,128]{2,1,0:T(8,128)(2,1)S(1)} %bitcast.49, bf16[16,64,128]{2,1,0:T(8,128)(2,1)S(1)} %bitcast.51, ...), custom_call_target="tpu_custom_call" | custom-call | flops 268435456 | bytes 8388608 | tf_op jit(solution)/shard_map/far_tiles/pallas_call | solution.py:255
  135.7 9.5 %all_to_all.44 = f32[16,16,128]{2,1,0:T(8,128)S(1)} all-to-all(f32[16,16,128]{2,1,0:T(8,128)S(1)} %bitcast.53), channel_id=1, replica_groups={{0,8,16,24,64,72,80,88,128,136,144,152,192,200,208,216},{1,9,17,25,65,7..., dimensions={0} | all-to-all | bytes 262144 | tf_op jit(solution)/shard_map/all_to_all | solution.py:65
  145.3 16.9 %all_to_all.45 = f32[16,16,128]{2,1,0:T(8,128)S(1)} all-to-all(f32[16,16,128]{2,1,0:T(8,128)S(1)} %broadcast_in_dim.16), channel_id=1, replica_groups={{0,1,2,3,4,5,6,7,32,33,34,35,36,37,38,39},{8,9,10,11,12,13,14,15,40,41,..., dimensions={0} | all-to-all | bytes 262144 | tf_op jit(solution)/shard_map/all_to_all | solution.py:48
  162.3 9.8 %all_to_all.46 = f32[16,16,128]{2,1,0:T(8,128)S(1)} all-to-all(f32[16,16,128]{2,1,0:T(8,128)S(1)} %broadcast_in_dim.17), channel_id=1, replica_groups={{0,8,16,24,64,72,80,88,128,136,144,152,192,200,208,216},{1,9,17,25,65,7..., dimensions={0} | all-to-all | bytes 262144 | tf_op jit(solution)/shard_map/all_to_all | solution.py:48
  172.1 4.9 %last_step.1 = (f32[2,64,512]{2,1,0:T(8,128)}, f32[2,64,64]{2,1,0:T(8,128)}) custom-call(f32[512,128]{1,0:T(8,128)S(1)} %bitcast.38, f32[256,128]{1,0:T(8,128)S(1)} %bitcast.39, f32[64,256]{1,0:T(8,128)S(1)} %get-tuple-element.61.cross, f32[64,512]{1,0:T(8,128)S(1)} %get-tuple-element.62.product, f32[256,512]{1,0:T(8,128)S(1)} %bitcast.34, ...), custom_call_target="tpu_custom_call" | custom-call | tf_op jit(solution)/shard_map/last_step/pallas_call | solution.py:421
  (55 shorter events, 16.4 us)
Async XLA Ops:
  2.5 27.0 %all-to-all-start = ((bf16[8,4,64,128]{3,2,1,0:T(8,128)(2,1)}), bf16[8,4,64,128]{3,2,1,0:T(8,128)(2,1)S(1)}, u32[]{:S(2)}, u32[]{:S(2)}) async-start(bf16[8,4,64,128]{3,2,1,0:T(8,128)(2,1)} %broadcast_in_dim.12), calls=%async_computation | async-start | bytes 1048576 | tf_op jit(solution)/shard_map/all_to_all | solution.py:48
  12.3 0.7 copy-start.4
  29.5 10.8 %collective-permute-start.1 = (bf16[4,4,64,128]{3,2,1,0:T(8,128)(2,1)S(1)}, bf16[4,4,64,128]{3,2,1,0:T(8,128)(2,1)S(1)}, u32[]{:S(2)}, u32[]{:S(2)}) collective-permute-start(bf16[4,4,64,128]{3,2,1,0:T(8,128)(2,1)S(1)} %get-tuple-element.66), channel_id=1, source_target_pairs={{0,24},{1,25},{2,26},{3,27},{4,28},{5,29},{6,30},{7,31},{8,0},{9,1... | collective-permute-start | bytes 786440 | tf_op jit(solution)/shard_map/ppermute | solution.py:53
  32.3 8.3 %collective-permute-start = (bf16[4,4,64,128]{3,2,1,0:T(8,128)(2,1)S(1)}, bf16[4,4,64,128]{3,2,1,0:T(8,128)(2,1)S(1)}, u32[]{:S(2)}, u32[]{:S(2)}) collective-permute-start(bf16[4,4,64,128]{3,2,1,0:T(8,128)(2,1)S(1)} %get-tuple-element.67), channel_id=1, source_target_pairs={{0,8},{1,9},{2,10},{3,11},{4,12},{5,13},{6,14},{7,15},{8,16},{9,17... | collective-permute-start | bytes 786440 | tf_op jit(solution)/shard_map/ppermute | solution.py:53
  32.4 13.8 %collective-permute-start.5 = (bf16[4,4,64,128]{3,2,1,0:T(8,128)(2,1)S(1)}, bf16[4,4,64,128]{3,2,1,0:T(8,128)(2,1)S(1)}, u32[]{:S(2)}, u32[]{:S(2)}) collective-permute-start(bf16[4,4,64,128]{3,2,1,0:T(8,128)(2,1)S(1)} %get-tuple-element.66), channel_id=1, source_target_pairs={{0,8},{1,9},{2,10},{3,11},{4,12},{5,13},{6,14},{7,15},{8,16},{9,17... | collective-permute-start | bytes 786440 | tf_op jit(solution)/shard_map/ppermute | solution.py:54
  32.5 13.7 %collective-permute-start.4 = (bf16[4,4,64,128]{3,2,1,0:T(8,128)(2,1)S(1)}, bf16[4,4,64,128]{3,2,1,0:T(8,128)(2,1)S(1)}, u32[]{:S(2)}, u32[]{:S(2)}) collective-permute-start(bf16[4,4,64,128]{3,2,1,0:T(8,128)(2,1)S(1)} %get-tuple-element.67), channel_id=1, source_target_pairs={{0,24},{1,25},{2,26},{3,27},{4,28},{5,29},{6,30},{7,31},{8,0},{9,1... | collective-permute-start | bytes 786440 | tf_op jit(solution)/shard_map/ppermute | solution.py:54
  35.3 3.4 %copy-start = (bf16[4,64,128,128]{3,2,1,0:T(8,128)(2,1)S(1)}, bf16[4,64,128,128]{3,2,1,0:T(8,128)(2,1)}, u32[]{:S(2)}) copy-start(bf16[4,64,128,128]{3,2,1,0:T(8,128)(2,1)} %param.4) | copy-start | bytes 25165828
  38.6 7.6 %copy-start.1 = (bf16[4,64,128,128]{3,2,1,0:T(8,128)(2,1)S(1)}, bf16[4,64,128,128]{3,2,1,0:T(8,128)(2,1)}, u32[]{:S(2)}) copy-start(bf16[4,64,128,128]{3,2,1,0:T(8,128)(2,1)} %param.4) | copy-start | bytes 25165828
  38.6 13.2 %copy-start.3 = (f32[4,64,512]{2,1,0:T(8,128)S(1)}, f32[4,64,512]{2,1,0:T(8,128)}, u32[]{:S(2)}) copy-start(f32[4,64,512]{2,1,0:T(8,128)} %param.7) | copy-start | bytes 1572868
  40.6 11.2 %collective-permute-start.2 = (bf16[4,4,64,128]{3,2,1,0:T(8,128)(2,1)S(1)}, bf16[4,4,64,128]{3,2,1,0:T(8,128)(2,1)S(1)}, u32[]{:S(2)}, u32[]{:S(2)}) collective-permute-start(bf16[4,4,64,128]{3,2,1,0:T(8,128)(2,1)S(1)} %collective-permute-done), channel_id=1, source_target_pairs={{0,8},{1,9},{2,10},{3,11},{4,12},{5,13},{6,14},{7,15},{8,16},{9,17... | collective-permute-start | bytes 786440 | tf_op jit(solution)/shard_map/ppermute | solution.py:59
  40.6 11.2 %collective-permute-start.3 = (bf16[4,4,64,128]{3,2,1,0:T(8,128)(2,1)S(1)}, bf16[4,4,64,128]{3,2,1,0:T(8,128)(2,1)S(1)}, u32[]{:S(2)}, u32[]{:S(2)}) collective-permute-start(bf16[4,4,64,128]{3,2,1,0:T(8,128)(2,1)S(1)} %collective-permute-done.1), channel_id=1, source_target_pairs={{0,24},{1,25},{2,26},{3,27},{4,28},{5,29},{6,30},{7,31},{8,0},{9,1... | collective-permute-start | bytes 786440 | tf_op jit(solution)/shard_map/ppermute | solution.py:59
  114.3 9.2 %collective-permute-start.7 = (bf16[4,4,64,128]{3,2,1,0:T(8,128)(2,1)S(1)}, bf16[4,4,64,128]{3,2,1,0:T(8,128)(2,1)S(1)}, u32[]{:S(2)}, u32[]{:S(2)}) collective-permute-start(bf16[4,4,64,128]{3,2,1,0:T(8,128)(2,1)S(1)} %get-tuple-element.64), channel_id=1, source_target_pairs={{0,24},{1,25},{2,26},{3,27},{4,28},{5,29},{6,30},{7,31},{8,0},{9,1... | collective-permute-start | bytes 786440 | tf_op jit(solution)/shard_map/ppermute | solution.py:53
  115.9 7.7 %collective-permute-start.6 = (bf16[4,4,64,128]{3,2,1,0:T(8,128)(2,1)S(1)}, bf16[4,4,64,128]{3,2,1,0:T(8,128)(2,1)S(1)}, u32[]{:S(2)}, u32[]{:S(2)}) collective-permute-start(bf16[4,4,64,128]{3,2,1,0:T(8,128)(2,1)S(1)} %get-tuple-element.65), channel_id=1, source_target_pairs={{0,8},{1,9},{2,10},{3,11},{4,12},{5,13},{6,14},{7,15},{8,16},{9,17... | collective-permute-start | bytes 786440 | tf_op jit(solution)/shard_map/ppermute | solution.py:53
  115.9 11.1 %collective-permute-start.11 = (bf16[4,4,64,128]{3,2,1,0:T(8,128)(2,1)S(1)}, bf16[4,4,64,128]{3,2,1,0:T(8,128)(2,1)S(1)}, u32[]{:S(2)}, u32[]{:S(2)}) collective-permute-start(bf16[4,4,64,128]{3,2,1,0:T(8,128)(2,1)S(1)} %get-tuple-element.64), channel_id=1, source_target_pairs={{0,8},{1,9},{2,10},{3,11},{4,12},{5,13},{6,14},{7,15},{8,16},{9,17... | collective-permute-start | bytes 786440 | tf_op jit(solution)/shard_map/ppermute | solution.py:54
  116.1 10.8 %collective-permute-start.10 = (bf16[4,4,64,128]{3,2,1,0:T(8,128)(2,1)S(1)}, bf16[4,4,64,128]{3,2,1,0:T(8,128)(2,1)S(1)}, u32[]{:S(2)}, u32[]{:S(2)}) collective-permute-start(bf16[4,4,64,128]{3,2,1,0:T(8,128)(2,1)S(1)} %get-tuple-element.65), channel_id=1, source_target_pairs={{0,24},{1,25},{2,26},{3,27},{4,28},{5,29},{6,30},{7,31},{8,0},{9,1... | collective-permute-start | bytes 786440 | tf_op jit(solution)/shard_map/ppermute | solution.py:54
  118.6 3.4 %copy-start.2 = (bf16[4,64,128,128]{3,2,1,0:T(8,128)(2,1)S(1)}, bf16[4,64,128,128]{3,2,1,0:T(8,128)(2,1)}, u32[]{:S(2)}) copy-start(bf16[4,64,128,128]{3,2,1,0:T(8,128)(2,1)} %param.4) | copy-start | bytes 25165828
  123.6 9.6 %collective-permute-start.8 = (bf16[4,4,64,128]{3,2,1,0:T(8,128)(2,1)S(1)}, bf16[4,4,64,128]{3,2,1,0:T(8,128)(2,1)S(1)}, u32[]{:S(2)}, u32[]{:S(2)}) collective-permute-start(bf16[4,4,64,128]{3,2,1,0:T(8,128)(2,1)S(1)} %collective-permute-done.6), channel_id=1, source_target_pairs={{0,8},{1,9},{2,10},{3,11},{4,12},{5,13},{6,14},{7,15},{8,16},{9,17... | collective-permute-start | bytes 786440 | tf_op jit(solution)/shard_map/ppermute | solution.py:59
  123.7 9.5 %collective-permute-start.9 = (bf16[4,4,64,128]{3,2,1,0:T(8,128)(2,1)S(1)}, bf16[4,4,64,128]{3,2,1,0:T(8,128)(2,1)S(1)}, u32[]{:S(2)}, u32[]{:S(2)}) collective-permute-start(bf16[4,4,64,128]{3,2,1,0:T(8,128)(2,1)S(1)} %collective-permute-done.7), channel_id=1, source_target_pairs={{0,24},{1,25},{2,26},{3,27},{4,28},{5,29},{6,30},{7,31},{8,0},{9,1... | collective-permute-start | bytes 786440 | tf_op jit(solution)/shard_map/ppermute | solution.py:59

commit v4 on v3

--- a/solution.py
+++ b/solution.py
@@ -10,7 +10,7 @@
 STEPS = 2
 NX, NY, NZ, NC = 4, 4, 8, 2
 SUB = 8
-PIVOTS = 4
+PIVOTS = 8
 GROUP, GROUP_BITS = 4, 2
 AT_ONCE, TRIP_BITS = 8, 5
 VECTORS, VECTOR_BITS = 32, 5
@@ -30,15 +30,14 @@
 Y_UP = [(col_id(y, z), col_id(y + 1, z)) for y in range(NY) for z in range(NZ)]
 Y_DOWN = [(col_id(y, z), col_id(y - 1, z)) for y in range(NY) for z in range(NZ)]
 Z_GROUPS = [[col_id(y, z) for z in range(NZ)] for y in range(NY)]
-XY_GROUPS = [
-    [row_id(x, c) * NY * NZ + col_id(y, z) for x in range(NX) for y in range(NY)]
-    for c in range(NC)
+PLANES = [
+    [
+        row_id(x, c) * NY * NZ + col_id(y, z)
+        for x in range(NX)
+        for y in range(NY)
+        for c in range(NC)
+    ]
     for z in range(NZ)
-]
-CZ_GROUPS = [
-    [row_id(x, c) * NY * NZ + col_id(y, z) for c in range(NC) for z in range(NZ)]
-    for x in range(NX)
-    for y in range(NY)
 ]
 ALL = ("row", "col")
 
@@ -46,6 +45,31 @@
 def to_all(a, axis, count, groups=None):
     copies = jnp.broadcast_to(a[None], (count,) + a.shape)
     return lax.all_to_all(copies, axis, 0, 0, axis_index_groups=groups, tiled=True)
+
+
+def spread_kernel(latest, out):
+    size = out.shape[3]
+    for i in range(out.shape[1]):
+        block = latest[0, :, i * size : (i + 1) * size].astype(out.dtype)
+        for n in range(out.shape[0]):
+            out[n, i] = block
+
+
+def spread_latest(earlier, size):
+    prev, b, rows = earlier.shape
+    out = (NZ, rows // size, b, size)
+    return pl.pallas_call(
+        spread_kernel,
+        out_shape=jax.ShapeDtypeStruct(out, jnp.bfloat16),
+        grid=(1,),
+        in_specs=[pl.BlockSpec((1, b, rows), lambda i: (prev - 1, 0, 0))],
+        out_specs=pl.BlockSpec(out, lambda i: (0, 0, 0, 0)),
+        name="spread_latest",
+    )(earlier)
+
+
+def along_z(copies):
+    return lax.all_to_all(copies, "col", 0, 0, axis_index_groups=Z_GROUPS, tiled=True)
 
 
 def gather_beside(own):
@@ -60,12 +84,12 @@
 
 
 def sum_everywhere(a):
-    members = NX * NY
+    members = NX * NY * NC
     part = a.reshape(members, a.shape[0] // members, a.shape[1])
-    piece = lax.all_to_all(part, ALL, 0, 0, axis_index_groups=XY_GROUPS, tiled=True)
+    piece = lax.all_to_all(part, ALL, 0, 0, axis_index_groups=PLANES, tiled=True)
     piece = jnp.sum(piece, 0)
-    piece = jnp.sum(to_all(piece, ALL, NC * NZ, CZ_GROUPS), 0)
-    return to_all(piece, ALL, members, XY_GROUPS).reshape(a.shape)
+    piece = jnp.sum(to_all(piece, "col", NZ, Z_GROUPS), 0)
+    return to_all(piece, ALL, members, PLANES).reshape(a.shape)
 
 
 def dot_nt(a, b):
@@ -344,9 +368,11 @@
     fresh[...] = new
     upper[...] = up
     cross[...] = dot_nn(inverse, proj - spread)
-    size = half.shape[2]
-    for i in range(half.shape[0]):
-        half[i] = new[:, i * size : (i + 1) * size].astype(half.dtype)
+    size = half.shape[3]
+    for i in range(half.shape[1]):
+        block = new[:, i * size : (i + 1) * size].astype(half.dtype)
+        for n in range(half.shape[0]):
+            half[n, i] = block
 
 
 def last_kernel(sums, later, cross, product, known, fresh, first_upper, out, uppers):
@@ -385,10 +411,7 @@
     known = earlier.reshape(prev * b, rows_here)
     prepared = prepare(picks, counts, slots)
 
-    def split(a):
-        return jnp.transpose(a.reshape(b, block_rows, size), (1, 0, 2))
-
-    own = to_all(split(earlier[-1].astype(jnp.bfloat16)), "col", NZ, Z_GROUPS)
+    own = along_z(spread_latest(earlier, size))
     own, prepared = lax.optimization_barrier((own, prepared))
     inner = jnp.dot(known, known.T, precision=HI) * scale
     blocks = [
@@ -403,7 +426,7 @@
         first_kernel,
         out_shape=(
             jax.ShapeDtypeStruct((b, rows_here), f32),
-            jax.ShapeDtypeStruct((block_rows, b, size), jnp.bfloat16),
+            jax.ShapeDtypeStruct((NZ, block_rows, b, size), jnp.bfloat16),
             jax.ShapeDtypeStruct((b, b), f32),
             jax.ShapeDtypeStruct((b, prev * b), f32),
         ),
@@ -413,7 +436,7 @@
         name="first_step",
     )(sums, product, known)
 
-    own = to_all(half, "col", NZ, Z_GROUPS)
+    own = along_z(half)
     basis = jnp.concatenate([known, fresh], 0)
     product, mixed = apply_tiles(tiles, prepared, own, basis, scale)
     mixed = jnp.concatenate([mixed, jnp.zeros((256 - mixed.shape[0], size), f32)], 0)

time: 179 us -> 177 us (0.989); the launches traced: 177 us -> 177 us
  waiting for transfers between devices: 22.2 us -> 24.3 us
  local copies, waits for them, and re-layouts: 9.79 us -> 7.81 us
    all_to_all x5 -> x4, blocking collectives: 71.4 us -> 44.8 us  [to_all(): lax.all_to_all(copies, axis, 0, 0, axis_index_groups=groups, tiled=True)]
    all_to_all x2 -> x3, blocking collectives: 20.7 us -> 47.1 us  [the longest x2 26.7 us: sum_everywhere(): lax.all_to_all(part, ALL, 0, 0, axis_index_groups=PLANES, tiled=True)]
    ppermute x4, waiting for transfers between devices: 3.25 us -> 5.61 us  [gather_beside(): rest = (lax.ppermute(last, 'col', Y_UP), lax.ppermute(first, 'col', Y_DOWN))]
  transfers between devices with their start and end apart: 13 -> 13, of which waited for: 6 -> 7; matrix products, arithmetic and copies ran while one was open for 2% -> 2% of each run, Pallas kernels for 6% -> 6%
where the time goes in v4:
time: 177 us
  blocking collectives  91.9 us (52%)
  Pallas kernels  24.8 us (14%)
  waiting for transfers between devices  24.3 us (14%)
  starting transfers between devices  24.2 us (14%)
  local copies, waits for them, and re-layouts  7.81 us (4%)
  matrix products  1.93 us (1%)
    all_to_all x4, blocking collectives, to_all(): lax.all_to_all(copies, axis, 0, 0, axis_index_groups=groups, tiled=True)  44.8 us
    all_to_all x2, blocking collectives, sum_everywhere(): lax.all_to_all(part, ALL, 0, 0, axis_index_groups=PLANES, tiled=True)  26.7 us
    all_to_all x1, blocking collectives, along_z(): lax.all_to_all(copies, 'col', 0, 0, axis_index_groups=Z_GROUPS, tiled=True)  20.4 us
    all_to_all x1, waiting for transfers between devices, along_z(): lax.all_to_all(copies, 'col', 0, 0, axis_index_groups=Z_GROUPS, tiled=True)  11.3 us
    all_to_all x1, starting transfers between devices, along_z(): lax.all_to_all(copies, 'col', 0, 0, axis_index_groups=Z_GROUPS, tiled=True)  9 us
    unnamed x13, local copies, waits for them, and re-layouts  7.51 us
    ppermute x2, waiting for transfers between devices, gather_beyond(): lax.ppermute(onward[0], 'col', Y_UP)  6.88 us
    ppermute x4, waiting for transfers between devices, gather_beside(): rest = (lax.ppermute(last, 'col', Y_UP), lax.ppermute(first, 'col', Y_DOWN))  5.61 us
  transfers between devices with their start and end apart: 13, of which 7 were waited for; matrix products, arithmetic and copies ran while one was open for 2% of the time, Pallas kernels for 6%

profile of v4, /device:TPU:1, one launch (start us, length us, event | category | flops | bytes accessed | tf_op | source)
XLA Modules:
  0.0 176.8 jit_solution(3323730579412576386)
XLA Ops:
  2.4 9.0 %all-to-all-start = ((bf16[8,4,64,128]{3,2,1,0:T(8,128)(2,1)}), bf16[8,4,64,128]{3,2,1,0:T(8,128)(2,1)S(1)}, u32[]{:S(2)}, u32[]{:S(2)}) async-start(bf16[8,4,64,128]{3,2,1,0:T(8,128)(2,1)} %spread_latest.1), calls=%async_computation | async-start | bytes 1048576 | tf_op jit(solution)/shard_map/all_to_all | solution.py:72
  12.8 3.3 %prepare.1 = (s32[336]{0:T(512)S(1)}, s32[336]{0:T(512)S(1)}, s32[336]{0:T(512)S(1)}, s32[84]{0:T(128)S(1)}, s32[84]{0:T(128)S(1)}, /*index=5*/s32[84]{0:T(128)S(1)}, s32[3]{0:T(128)S(1)}) custom-call(s32[256]{0:T(256)S(1)} %reshape.76.picks, s32[4]{0:T(128)S(1)} %bitcast.52), custom_call_target="tpu_custom_call" | custom-call | bytes 8388608 | tf_op jit(solution)/shard_map/prepare/pallas_call | solution.py:155
  18.1 11.3 %all-to-all-done = bf16[8,4,64,128]{3,2,1,0:T(8,128)(2,1)S(1)} async-done(((bf16[8,4,64,128]{3,2,1,0:T(8,128)(2,1)}), bf16[8,4,64,128]{3,2,1,0:T(8,128)(2,1)S(1)}, u32[]{:S(2)}, u32[]{:S(2)}) %all-to-all-start) | async-done | bytes 524320 | tf_op jit(solution)/shard_map/all_to_all | solution.py:72
  29.4 2.8 %collective-permute-start.1 = (bf16[4,4,64,128]{3,2,1,0:T(8,128)(2,1)S(1)}, bf16[4,4,64,128]{3,2,1,0:T(8,128)(2,1)S(1)}, u32[]{:S(2)}, u32[]{:S(2)}) collective-permute-start(bf16[4,4,64,128]{3,2,1,0:T(8,128)(2,1)S(1)} %get-tuple-element.66), channel_id=1, source_target_pairs={{0,24},{1,25},{2,26},{3,27},{4,28},{5,29},{6,30},{7,31},{8,0},{9,1... | collective-permute-start | bytes 786440 | tf_op jit(solution)/shard_map/ppermute | solution.py:77
  32.4 2.7 %collective-permute-start.4 = (bf16[4,4,64,128]{3,2,1,0:T(8,128)(2,1)S(1)}, bf16[4,4,64,128]{3,2,1,0:T(8,128)(2,1)S(1)}, u32[]{:S(2)}, u32[]{:S(2)}) collective-permute-start(bf16[4,4,64,128]{3,2,1,0:T(8,128)(2,1)S(1)} %get-tuple-element.67), channel_id=1, source_target_pairs={{0,24},{1,25},{2,26},{3,27},{4,28},{5,29},{6,30},{7,31},{8,0},{9,1... | collective-permute-start | bytes 786440 | tf_op jit(solution)/shard_map/ppermute | solution.py:78
  35.1 3.4 %copy-done = bf16[4,64,128,128]{3,2,1,0:T(8,128)(2,1)S(1)} copy-done((bf16[4,64,128,128]{3,2,1,0:T(8,128)(2,1)S(1)}, bf16[4,64,128,128]{3,2,1,0:T(8,128)(2,1)}, u32[]{:S(2)}) %copy-start) | copy-done | bytes 8388632
  40.5 2.7 %collective-permute-start.3 = (bf16[4,4,64,128]{3,2,1,0:T(8,128)(2,1)S(1)}, bf16[4,4,64,128]{3,2,1,0:T(8,128)(2,1)S(1)}, u32[]{:S(2)}, u32[]{:S(2)}) collective-permute-start(bf16[4,4,64,128]{3,2,1,0:T(8,128)(2,1)S(1)} %collective-permute-done.1), channel_id=1, source_target_pairs={{0,24},{1,25},{2,26},{3,27},{4,28},{5,29},{6,30},{7,31},{8,0},{9,1... | collective-permute-start | bytes 786440 | tf_op jit(solution)/shard_map/ppermute | solution.py:83
  43.4 2.7 %collective-permute-done.5 = bf16[4,4,64,128]{3,2,1,0:T(8,128)(2,1)S(1)} collective-permute-done((bf16[4,4,64,128]{3,2,1,0:T(8,128)(2,1)S(1)}, bf16[4,4,64,128]{3,2,1,0:T(8,128)(2,1)S(1)}, u32[]{:S(2)}, u32[]{:S(2)}) %collective-permute-start.5) | collective-permute-done | bytes 262176 | tf_op jit(solution)/shard_map/ppermute | solution.py:78
  48.3 3.4 %collective-permute-done.2 = bf16[4,4,64,128]{3,2,1,0:T(8,128)(2,1)S(1)} collective-permute-done((bf16[4,4,64,128]{3,2,1,0:T(8,128)(2,1)S(1)}, bf16[4,4,64,128]{3,2,1,0:T(8,128)(2,1)S(1)}, u32[]{:S(2)}, u32[]{:S(2)}) %collective-permute-start.2) | collective-permute-done | bytes 262176 | tf_op jit(solution)/shard_map/ppermute | solution.py:83
  54.1 14.9 %all_to_all.40 = f32[32,16,128]{2,1,0:T(8,128)S(1)} all-to-all(f32[32,16,128]{2,1,0:T(8,128)S(1)} %bitcast.53), channel_id=1, replica_groups={{0,32,8,40,16,48,24,56,64,96,72,104,80,112,88,120,128,160,136,168,144,1..., dimensions={0} | all-to-all | bytes 524288 | tf_op jit(solution)/shard_map/all_to_all | solution.py:89
  69.0 9.5 %all_to_all.41 = f32[8,16,128]{2,1,0:T(8,128)S(1)} all-to-all(f32[8,16,128]{2,1,0:T(8,128)S(1)} %broadcast_in_dim.8), channel_id=1, replica_groups={{0,1,2,3,4,5,6,7},{8,9,10,11,12,13,14,15},{16,17,18,19,20,21,22,23},{24..., dimensions={0} | all-to-all | bytes 131072 | tf_op jit(solution)/shard_map/all_to_all | solution.py:47
  78.6 13.7 %all_to_all.42 = f32[32,16,128]{2,1,0:T(8,128)S(1)} all-to-all(f32[32,16,128]{2,1,0:T(8,128)S(1)} %broadcast_in_dim.9), channel_id=1, replica_groups={{0,32,8,40,16,48,24,56,64,96,72,104,80,112,88,120,128,160,136,168,144,1..., dimensions={0} | all-to-all | bytes 524288 | tf_op jit(solution)/shard_map/all_to_all | solution.py:47
  92.2 3.2 %first_step.1 = (f32[64,512]{1,0:T(8,128)S(1)}, bf16[8,4,64,128]{3,2,1,0:T(8,128)(2,1)S(1)}, f32[64,64]{1,0:T(8,128)S(1)}, f32[64,256]{1,0:T(8,128)S(1)}) custom-call(f32[512,128]{1,0:T(8,128)S(1)} %bitcast.37, f32[64,512]{1,0:T(8,128)S(1)} %get-tuple-element.54.product, f32[256,512]{1,0:T(8,128)S(1)} %bitcast.32), custom_call_target="tpu_custom_call" | custom-call | tf_op jit(solution)/shard_map/first_step/pallas_call | solution.py:425
  95.5 20.4 %all_to_all.43 = bf16[8,4,64,128]{3,2,1,0:T(8,128)(2,1)S(1)} all-to-all(bf16[8,4,64,128]{3,2,1,0:T(8,128)(2,1)S(1)} %get-tuple-element.55), channel_id=1, replica_groups={{0,1,2,3,4,5,6,7},{8,9,10,11,12,13,14,15},{16,17,18,19,20,21,22,23},{24..., dimensions={0} | all-to-all | bytes 1048576 | tf_op jit(solution)/shard_map/all_to_all | solution.py:72
  117.7 2.4 %collective-permute-start.10 = (bf16[4,4,64,128]{3,2,1,0:T(8,128)(2,1)S(1)}, bf16[4,4,64,128]{3,2,1,0:T(8,128)(2,1)S(1)}, u32[]{:S(2)}, u32[]{:S(2)}) collective-permute-start(bf16[4,4,64,128]{3,2,1,0:T(8,128)(2,1)S(1)} %get-tuple-element.65), channel_id=1, source_target_pairs={{0,24},{1,25},{2,26},{3,27},{4,28},{5,29},{6,30},{7,31},{8,0},{9,1... | collective-permute-start | bytes 786440 | tf_op jit(solution)/shard_map/ppermute | solution.py:78
  120.1 3.4 %copy-done.2 = bf16[4,64,128,128]{3,2,1,0:T(8,128)(2,1)S(1)} copy-done((bf16[4,64,128,128]{3,2,1,0:T(8,128)(2,1)S(1)}, bf16[4,64,128,128]{3,2,1,0:T(8,128)(2,1)}, u32[]{:S(2)}) %copy-start.2) | copy-done | bytes 8388632
  125.3 2.7 %collective-permute-start.9 = (bf16[4,4,64,128]{3,2,1,0:T(8,128)(2,1)S(1)}, bf16[4,4,64,128]{3,2,1,0:T(8,128)(2,1)S(1)}, u32[]{:S(2)}, u32[]{:S(2)}) collective-permute-start(bf16[4,4,64,128]{3,2,1,0:T(8,128)(2,1)S(1)} %collective-permute-done.7), channel_id=1, source_target_pairs={{0,24},{1,25},{2,26},{3,27},{4,28},{5,29},{6,30},{7,31},{8,0},{9,1... | collective-permute-start | bytes 786440 | tf_op jit(solution)/shard_map/ppermute | solution.py:83
  128.0 2.9 %collective-permute-done.11 = bf16[4,4,64,128]{3,2,1,0:T(8,128)(2,1)S(1)} collective-permute-done((bf16[4,4,64,128]{3,2,1,0:T(8,128)(2,1)S(1)}, bf16[4,4,64,128]{3,2,1,0:T(8,128)(2,1)S(1)}, u32[]{:S(2)}, u32[]{:S(2)}) %collective-permute-start.11) | collective-permute-done | bytes 262176 | tf_op jit(solution)/shard_map/ppermute | solution.py:78
  133.1 3.4 %collective-permute-done.8 = bf16[4,4,64,128]{3,2,1,0:T(8,128)(2,1)S(1)} collective-permute-done((bf16[4,4,64,128]{3,2,1,0:T(8,128)(2,1)S(1)}, bf16[4,4,64,128]{3,2,1,0:T(8,128)(2,1)S(1)}, u32[]{:S(2)}, u32[]{:S(2)}) %collective-permute-start.8) | collective-permute-done | bytes 262176 | tf_op jit(solution)/shard_map/ppermute | solution.py:83
  136.6 2.5 %far_tiles.3 = (f32[64,512]{1,0:T(8,128)S(1)}, f32[192,128]{1,0:T(8,128)S(1)}) custom-call(s32[336]{0:T(512)S(1)} %get-tuple-element.40.table, s32[84]{0:T(128)S(1)} %get-tuple-element.41.rows, s32[3]{0:T(128)S(1)} %get-tuple-element.51.totals, bf16[16,64,128]{2,1,0:T(8,128)(2,1)S(1)} %bitcast.49, bf16[16,64,128]{2,1,0:T(8,128)(2,1)S(1)} %bitcast.51, ...), custom_call_target="tpu_custom_call" | custom-call | flops 268435456 | bytes 8388608 | tf_op jit(solution)/shard_map/far_tiles/pallas_call | solution.py:279
  139.1 11.8 %all_to_all.44 = f32[32,8,128]{2,1,0:T(8,128)S(1)} all-to-all(f32[32,8,128]{2,1,0:T(8,128)S(1)} %pad_bitcast_fusion), channel_id=1, replica_groups={{0,32,8,40,16,48,24,56,64,96,72,104,80,112,88,120,128,160,136,168,144,1..., dimensions={0} | all-to-all | bytes 262144 | tf_op jit(solution)/shard_map/all_to_all | solution.py:89
  150.9 9.2 %all_to_all.45 = f32[8,8,128]{2,1,0:T(8,128)S(1)} all-to-all(f32[8,8,128]{2,1,0:T(8,128)S(1)} %broadcast_in_dim.10), channel_id=1, replica_groups={{0,1,2,3,4,5,6,7},{8,9,10,11,12,13,14,15},{16,17,18,19,20,21,22,23},{24..., dimensions={0} | all-to-all | bytes 65536 | tf_op jit(solution)/shard_map/all_to_all | solution.py:47
  160.2 12.4 %all_to_all.46 = f32[32,8,128]{2,1,0:T(8,128)S(1)} all-to-all(f32[32,8,128]{2,1,0:T(8,128)S(1)} %broadcast_in_dim.11), channel_id=1, replica_groups={{0,32,8,40,16,48,24,56,64,96,72,104,80,112,88,120,128,160,136,168,144,1..., dimensions={0} | all-to-all | bytes 262144 | tf_op jit(solution)/shard_map/all_to_all | solution.py:47
  172.6 4.2 %last_step.1 = (f32[2,64,512]{2,1,0:T(8,128)}, f32[2,64,64]{2,1,0:T(8,128)}) custom-call(f32[512,128]{1,0:T(8,128)S(1)} %bitcast.38, f32[256,128]{1,0:T(8,128)S(1)} %bitcast.39, f32[64,256]{1,0:T(8,128)S(1)} %get-tuple-element.61.cross, f32[64,512]{1,0:T(8,128)S(1)} %get-tuple-element.62.product, f32[256,512]{1,0:T(8,128)S(1)} %bitcast.34, ...), custom_call_target="tpu_custom_call" | custom-call | tf_op jit(solution)/shard_map/last_step/pallas_call | solution.py:444
  (51 shorter events, 18.0 us)
Async XLA Ops:
  2.4 27.0 %all-to-all-start = ((bf16[8,4,64,128]{3,2,1,0:T(8,128)(2,1)}), bf16[8,4,64,128]{3,2,1,0:T(8,128)(2,1)S(1)}, u32[]{:S(2)}, u32[]{:S(2)}) async-start(bf16[8,4,64,128]{3,2,1,0:T(8,128)(2,1)} %spread_latest.1), calls=%async_computation | async-start | bytes 1048576 | tf_op jit(solution)/shard_map/all_to_all | solution.py:72
  12.2 0.7 copy-start.4
  29.4 10.8 %collective-permute-start.1 = (bf16[4,4,64,128]{3,2,1,0:T(8,128)(2,1)S(1)}, bf16[4,4,64,128]{3,2,1,0:T(8,128)(2,1)S(1)}, u32[]{:S(2)}, u32[]{:S(2)}) collective-permute-start(bf16[4,4,64,128]{3,2,1,0:T(8,128)(2,1)S(1)} %get-tuple-element.66), channel_id=1, source_target_pairs={{0,24},{1,25},{2,26},{3,27},{4,28},{5,29},{6,30},{7,31},{8,0},{9,1... | collective-permute-start | bytes 786440 | tf_op jit(solution)/shard_map/ppermute | solution.py:77
  32.2 8.3 %collective-permute-start = (bf16[4,4,64,128]{3,2,1,0:T(8,128)(2,1)S(1)}, bf16[4,4,64,128]{3,2,1,0:T(8,128)(2,1)S(1)}, u32[]{:S(2)}, u32[]{:S(2)}) collective-permute-start(bf16[4,4,64,128]{3,2,1,0:T(8,128)(2,1)S(1)} %get-tuple-element.67), channel_id=1, source_target_pairs={{0,8},{1,9},{2,10},{3,11},{4,12},{5,13},{6,14},{7,15},{8,16},{9,17... | collective-permute-start | bytes 786440 | tf_op jit(solution)/shard_map/ppermute | solution.py:77
  32.3 13.8 %collective-permute-start.5 = (bf16[4,4,64,128]{3,2,1,0:T(8,128)(2,1)S(1)}, bf16[4,4,64,128]{3,2,1,0:T(8,128)(2,1)S(1)}, u32[]{:S(2)}, u32[]{:S(2)}) collective-permute-start(bf16[4,4,64,128]{3,2,1,0:T(8,128)(2,1)S(1)} %get-tuple-element.66), channel_id=1, source_target_pairs={{0,8},{1,9},{2,10},{3,11},{4,12},{5,13},{6,14},{7,15},{8,16},{9,17... | collective-permute-start | bytes 786440 | tf_op jit(solution)/shard_map/ppermute | solution.py:78
  32.4 13.7 %collective-permute-start.4 = (bf16[4,4,64,128]{3,2,1,0:T(8,128)(2,1)S(1)}, bf16[4,4,64,128]{3,2,1,0:T(8,128)(2,1)S(1)}, u32[]{:S(2)}, u32[]{:S(2)}) collective-permute-start(bf16[4,4,64,128]{3,2,1,0:T(8,128)(2,1)S(1)} %get-tuple-element.67), channel_id=1, source_target_pairs={{0,24},{1,25},{2,26},{3,27},{4,28},{5,29},{6,30},{7,31},{8,0},{9,1... | collective-permute-start | bytes 786440 | tf_op jit(solution)/shard_map/ppermute | solution.py:78
  35.1 3.4 %copy-start = (bf16[4,64,128,128]{3,2,1,0:T(8,128)(2,1)S(1)}, bf16[4,64,128,128]{3,2,1,0:T(8,128)(2,1)}, u32[]{:S(2)}) copy-start(bf16[4,64,128,128]{3,2,1,0:T(8,128)(2,1)} %param.4) | copy-start | bytes 25165828
  38.5 7.6 %copy-start.1 = (bf16[4,64,128,128]{3,2,1,0:T(8,128)(2,1)S(1)}, bf16[4,64,128,128]{3,2,1,0:T(8,128)(2,1)}, u32[]{:S(2)}) copy-start(bf16[4,64,128,128]{3,2,1,0:T(8,128)(2,1)} %param.4) | copy-start | bytes 25165828
  38.5 13.2 %copy-start.3 = (f32[4,64,512]{2,1,0:T(8,128)S(1)}, f32[4,64,512]{2,1,0:T(8,128)}, u32[]{:S(2)}) copy-start(f32[4,64,512]{2,1,0:T(8,128)} %latest.1) | copy-start | bytes 1572868
  40.5 11.2 %collective-permute-start.2 = (bf16[4,4,64,128]{3,2,1,0:T(8,128)(2,1)S(1)}, bf16[4,4,64,128]{3,2,1,0:T(8,128)(2,1)S(1)}, u32[]{:S(2)}, u32[]{:S(2)}) collective-permute-start(bf16[4,4,64,128]{3,2,1,0:T(8,128)(2,1)S(1)} %collective-permute-done), channel_id=1, source_target_pairs={{0,8},{1,9},{2,10},{3,11},{4,12},{5,13},{6,14},{7,15},{8,16},{9,17... | collective-permute-start | bytes 786440 | tf_op jit(solution)/shard_map/ppermute | solution.py:83
  40.5 11.2 %collective-permute-start.3 = (bf16[4,4,64,128]{3,2,1,0:T(8,128)(2,1)S(1)}, bf16[4,4,64,128]{3,2,1,0:T(8,128)(2,1)S(1)}, u32[]{:S(2)}, u32[]{:S(2)}) collective-permute-start(bf16[4,4,64,128]{3,2,1,0:T(8,128)(2,1)S(1)} %collective-permute-done.1), channel_id=1, source_target_pairs={{0,24},{1,25},{2,26},{3,27},{4,28},{5,29},{6,30},{7,31},{8,0},{9,1... | collective-permute-start | bytes 786440 | tf_op jit(solution)/shard_map/ppermute | solution.py:83
  115.9 9.2 %collective-permute-start.7 = (bf16[4,4,64,128]{3,2,1,0:T(8,128)(2,1)S(1)}, bf16[4,4,64,128]{3,2,1,0:T(8,128)(2,1)S(1)}, u32[]{:S(2)}, u32[]{:S(2)}) collective-permute-start(bf16[4,4,64,128]{3,2,1,0:T(8,128)(2,1)S(1)} %get-tuple-element.64), channel_id=1, source_target_pairs={{0,24},{1,25},{2,26},{3,27},{4,28},{5,29},{6,30},{7,31},{8,0},{9,1... | collective-permute-start | bytes 786440 | tf_op jit(solution)/shard_map/ppermute | solution.py:77
  117.0 8.3 %collective-permute-start.6 = (bf16[4,4,64,128]{3,2,1,0:T(8,128)(2,1)S(1)}, bf16[4,4,64,128]{3,2,1,0:T(8,128)(2,1)S(1)}, u32[]{:S(2)}, u32[]{:S(2)}) collective-permute-start(bf16[4,4,64,128]{3,2,1,0:T(8,128)(2,1)S(1)} %get-tuple-element.65), channel_id=1, source_target_pairs={{0,8},{1,9},{2,10},{3,11},{4,12},{5,13},{6,14},{7,15},{8,16},{9,17... | collective-permute-start | bytes 786440 | tf_op jit(solution)/shard_map/ppermute | solution.py:77
  117.5 13.5 %collective-permute-start.11 = (bf16[4,4,64,128]{3,2,1,0:T(8,128)(2,1)S(1)}, bf16[4,4,64,128]{3,2,1,0:T(8,128)(2,1)S(1)}, u32[]{:S(2)}, u32[]{:S(2)}) collective-permute-start(bf16[4,4,64,128]{3,2,1,0:T(8,128)(2,1)S(1)} %get-tuple-element.64), channel_id=1, source_target_pairs={{0,8},{1,9},{2,10},{3,11},{4,12},{5,13},{6,14},{7,15},{8,16},{9,17... | collective-permute-start | bytes 786440 | tf_op jit(solution)/shard_map/ppermute | solution.py:78
  117.7 13.2 %collective-permute-start.10 = (bf16[4,4,64,128]{3,2,1,0:T(8,128)(2,1)S(1)}, bf16[4,4,64,128]{3,2,1,0:T(8,128)(2,1)S(1)}, u32[]{:S(2)}, u32[]{:S(2)}) collective-permute-start(bf16[4,4,64,128]{3,2,1,0:T(8,128)(2,1)S(1)} %get-tuple-element.65), channel_id=1, source_target_pairs={{0,24},{1,25},{2,26},{3,27},{4,28},{5,29},{6,30},{7,31},{8,0},{9,1... | collective-permute-start | bytes 786440 | tf_op jit(solution)/shard_map/ppermute | solution.py:78
  120.1 3.4 %copy-start.2 = (bf16[4,64,128,128]{3,2,1,0:T(8,128)(2,1)S(1)}, bf16[4,64,128,128]{3,2,1,0:T(8,128)(2,1)}, u32[]{:S(2)}) copy-start(bf16[4,64,128,128]{3,2,1,0:T(8,128)(2,1)} %param.4) | copy-start | bytes 25165828
  125.3 11.2 %collective-permute-start.8 = (bf16[4,4,64,128]{3,2,1,0:T(8,128)(2,1)S(1)}, bf16[4,4,64,128]{3,2,1,0:T(8,128)(2,1)S(1)}, u32[]{:S(2)}, u32[]{:S(2)}) collective-permute-start(bf16[4,4,64,128]{3,2,1,0:T(8,128)(2,1)S(1)} %collective-permute-done.6), channel_id=1, source_target_pairs={{0,8},{1,9},{2,10},{3,11},{4,12},{5,13},{6,14},{7,15},{8,16},{9,17... | collective-permute-start | bytes 786440 | tf_op jit(solution)/shard_map/ppermute | solution.py:83
  125.3 11.2 %collective-permute-start.9 = (bf16[4,4,64,128]{3,2,1,0:T(8,128)(2,1)S(1)}, bf16[4,4,64,128]{3,2,1,0:T(8,128)(2,1)S(1)}, u32[]{:S(2)}, u32[]{:S(2)}) collective-permute-start(bf16[4,4,64,128]{3,2,1,0:T(8,128)(2,1)S(1)} %collective-permute-done.7), channel_id=1, source_target_pairs={{0,24},{1,25},{2,26},{3,27},{4,28},{5,29},{6,30},{7,31},{8,0},{9,1... | collective-permute-start | bytes 786440 | tf_op jit(solution)/shard_map/ppermute | solution.py:83

commit v5 on v4

--- a/solution.py
+++ b/solution.py
@@ -381,13 +381,11 @@
     own = known_inner(sums, prev, b)
     old = jnp.concatenate([block_of(later, i, b) for i in range(prev)], 1)
     new = block_of(later, prev, b)
-    spread = dot_nn(old, own) + dot_nn(new, cross[...])
+    proj = jnp.concatenate([old, new], 1)
+    spread = dot_nn(proj, jnp.concatenate([own, cross[...]], 0))
     spread_new = dot_nt(old, cross[...]) + new
-    gram = (
-        block_of(later, prev + 1, b)
-        + dot_nt(spread - 2.0 * old, old)
-        + dot_nt(spread_new - 2.0 * new, new)
-    )
+    spread = jnp.concatenate([spread, spread_new], 1)
+    gram = block_of(later, prev + 1, b) + dot_nt(spread - 2.0 * proj, proj)
     residual = product[...] - dot_nn(old, known[...]) - dot_nn(new, fresh[...])
     up, inverse = factor(gram)
     out[0] = fresh[...]

time: 177 us -> 178 us (level)
  transfers between devices with their start and end apart: 13 -> 13, of which waited for: 7 -> 7; matrix products, arithmetic and copies ran while one was open for 2% -> 2% of each run, Pallas kernels for 6% -> 5%
where the time goes in v5:
time: 178 us; the launch traced here: 177 us
  blocking collectives  92.3 us (52%)
  waiting for transfers between devices  25.5 us (14%)
  starting transfers between devices  24.2 us (14%)
  Pallas kernels  23.7 us (13%)
  local copies, waits for them, and re-layouts  7.81 us (4%)
  matrix products  1.93 us (1%)
    all_to_all x4, blocking collectives, to_all(): lax.all_to_all(copies, axis, 0, 0, axis_index_groups=groups, tiled=True)  44.8 us
    all_to_all x2, blocking collectives, sum_everywhere(): lax.all_to_all(part, ALL, 0, 0, axis_index_groups=PLANES, tiled=True)  27.1 us
    all_to_all x1, blocking collectives, along_z(): lax.all_to_all(copies, 'col', 0, 0, axis_index_groups=Z_GROUPS, tiled=True)  20.4 us
    all_to_all x1, waiting for transfers between devices, along_z(): lax.all_to_all(copies, 'col', 0, 0, axis_index_groups=Z_GROUPS, tiled=True)  11.5 us
    all_to_all x1, starting transfers between devices, along_z(): lax.all_to_all(copies, 'col', 0, 0, axis_index_groups=Z_GROUPS, tiled=True)  9 us
    ppermute x2, waiting for transfers between devices, gather_beyond(): lax.ppermute(onward[0], 'col', Y_UP)  7.86 us
    unnamed x13, local copies, waits for them, and re-layouts  7.51 us
    ppermute x4, waiting for transfers between devices, gather_beside(): rest = (lax.ppermute(last, 'col', Y_UP), lax.ppermute(first, 'col', Y_DOWN))  5.61 us
  transfers between devices with their start and end apart: 13, of which 7 were waited for; matrix products, arithmetic and copies ran while one was open for 2% of the time, Pallas kernels for 5%

profile of v5, /device:TPU:1, one launch (start us, length us, event | category | flops | bytes accessed | tf_op | source)
XLA Modules:
  0.0 177.3 jit_solution(12665835920025372377)
XLA Ops:
  2.4 9.0 %all-to-all-start = ((bf16[8,4,64,128]{3,2,1,0:T(8,128)(2,1)}), bf16[8,4,64,128]{3,2,1,0:T(8,128)(2,1)S(1)}, u32[]{:S(2)}, u32[]{:S(2)}) async-start(bf16[8,4,64,128]{3,2,1,0:T(8,128)(2,1)} %spread_latest.1), calls=%async_computation | async-start | bytes 1048576 | tf_op jit(solution)/shard_map/all_to_all | solution.py:72
  12.8 3.1 %prepare.1 = (s32[336]{0:T(512)S(1)}, s32[336]{0:T(512)S(1)}, s32[336]{0:T(512)S(1)}, s32[84]{0:T(128)S(1)}, s32[84]{0:T(128)S(1)}, /*index=5*/s32[84]{0:T(128)S(1)}, s32[3]{0:T(128)S(1)}) custom-call(s32[256]{0:T(256)S(1)} %reshape.76.picks, s32[4]{0:T(128)S(1)} %bitcast.52), custom_call_target="tpu_custom_call" | custom-call | bytes 8388608 | tf_op jit(solution)/shard_map/prepare/pallas_call | solution.py:155
  17.8 11.5 %all-to-all-done = bf16[8,4,64,128]{3,2,1,0:T(8,128)(2,1)S(1)} async-done(((bf16[8,4,64,128]{3,2,1,0:T(8,128)(2,1)}), bf16[8,4,64,128]{3,2,1,0:T(8,128)(2,1)S(1)}, u32[]{:S(2)}, u32[]{:S(2)}) %all-to-all-start) | async-done | bytes 524320 | tf_op jit(solution)/shard_map/all_to_all | solution.py:72
  29.4 2.8 %collective-permute-start.1 = (bf16[4,4,64,128]{3,2,1,0:T(8,128)(2,1)S(1)}, bf16[4,4,64,128]{3,2,1,0:T(8,128)(2,1)S(1)}, u32[]{:S(2)}, u32[]{:S(2)}) collective-permute-start(bf16[4,4,64,128]{3,2,1,0:T(8,128)(2,1)S(1)} %get-tuple-element.66), channel_id=1, source_target_pairs={{0,24},{1,25},{2,26},{3,27},{4,28},{5,29},{6,30},{7,31},{8,0},{9,1... | collective-permute-start | bytes 786440 | tf_op jit(solution)/shard_map/ppermute | solution.py:77
  32.4 2.7 %collective-permute-start.4 = (bf16[4,4,64,128]{3,2,1,0:T(8,128)(2,1)S(1)}, bf16[4,4,64,128]{3,2,1,0:T(8,128)(2,1)S(1)}, u32[]{:S(2)}, u32[]{:S(2)}) collective-permute-start(bf16[4,4,64,128]{3,2,1,0:T(8,128)(2,1)S(1)} %get-tuple-element.67), channel_id=1, source_target_pairs={{0,24},{1,25},{2,26},{3,27},{4,28},{5,29},{6,30},{7,31},{8,0},{9,1... | collective-permute-start | bytes 786440 | tf_op jit(solution)/shard_map/ppermute | solution.py:78
  35.1 3.4 %copy-done = bf16[4,64,128,128]{3,2,1,0:T(8,128)(2,1)S(1)} copy-done((bf16[4,64,128,128]{3,2,1,0:T(8,128)(2,1)S(1)}, bf16[4,64,128,128]{3,2,1,0:T(8,128)(2,1)}, u32[]{:S(2)}) %copy-start) | copy-done | bytes 8388632
  40.5 2.7 %collective-permute-start.3 = (bf16[4,4,64,128]{3,2,1,0:T(8,128)(2,1)S(1)}, bf16[4,4,64,128]{3,2,1,0:T(8,128)(2,1)S(1)}, u32[]{:S(2)}, u32[]{:S(2)}) collective-permute-start(bf16[4,4,64,128]{3,2,1,0:T(8,128)(2,1)S(1)} %collective-permute-done.1), channel_id=1, source_target_pairs={{0,24},{1,25},{2,26},{3,27},{4,28},{5,29},{6,30},{7,31},{8,0},{9,1... | collective-permute-start | bytes 786440 | tf_op jit(solution)/shard_map/ppermute | solution.py:83
  43.4 2.7 %collective-permute-done.5 = bf16[4,4,64,128]{3,2,1,0:T(8,128)(2,1)S(1)} collective-permute-done((bf16[4,4,64,128]{3,2,1,0:T(8,128)(2,1)S(1)}, bf16[4,4,64,128]{3,2,1,0:T(8,128)(2,1)S(1)}, u32[]{:S(2)}, u32[]{:S(2)}) %collective-permute-start.5) | collective-permute-done | bytes 262176 | tf_op jit(solution)/shard_map/ppermute | solution.py:78
  47.8 3.9 %collective-permute-done.2 = bf16[4,4,64,128]{3,2,1,0:T(8,128)(2,1)S(1)} collective-permute-done((bf16[4,4,64,128]{3,2,1,0:T(8,128)(2,1)S(1)}, bf16[4,4,64,128]{3,2,1,0:T(8,128)(2,1)S(1)}, u32[]{:S(2)}, u32[]{:S(2)}) %collective-permute-start.2) | collective-permute-done | bytes 262176 | tf_op jit(solution)/shard_map/ppermute | solution.py:83
  54.1 15.1 %all_to_all.40 = f32[32,16,128]{2,1,0:T(8,128)S(1)} all-to-all(f32[32,16,128]{2,1,0:T(8,128)S(1)} %bitcast.53), channel_id=1, replica_groups={{0,32,8,40,16,48,24,56,64,96,72,104,80,112,88,120,128,160,136,168,144,1..., dimensions={0} | all-to-all | bytes 524288 | tf_op jit(solution)/shard_map/all_to_all | solution.py:89
  69.2 9.5 %all_to_all.41 = f32[8,16,128]{2,1,0:T(8,128)S(1)} all-to-all(f32[8,16,128]{2,1,0:T(8,128)S(1)} %broadcast_in_dim.8), channel_id=1, replica_groups={{0,1,2,3,4,5,6,7},{8,9,10,11,12,13,14,15},{16,17,18,19,20,21,22,23},{24..., dimensions={0} | all-to-all | bytes 131072 | tf_op jit(solution)/shard_map/all_to_all | solution.py:47
  78.8 13.7 %all_to_all.42 = f32[32,16,128]{2,1,0:T(8,128)S(1)} all-to-all(f32[32,16,128]{2,1,0:T(8,128)S(1)} %broadcast_in_dim.9), channel_id=1, replica_groups={{0,32,8,40,16,48,24,56,64,96,72,104,80,112,88,120,128,160,136,168,144,1..., dimensions={0} | all-to-all | bytes 524288 | tf_op jit(solution)/shard_map/all_to_all | solution.py:47
  92.5 3.2 %first_step.1 = (f32[64,512]{1,0:T(8,128)S(1)}, bf16[8,4,64,128]{3,2,1,0:T(8,128)(2,1)S(1)}, f32[64,64]{1,0:T(8,128)S(1)}, f32[64,256]{1,0:T(8,128)S(1)}) custom-call(f32[512,128]{1,0:T(8,128)S(1)} %bitcast.37, f32[64,512]{1,0:T(8,128)S(1)} %get-tuple-element.54.product, f32[256,512]{1,0:T(8,128)S(1)} %bitcast.32), custom_call_target="tpu_custom_call" | custom-call | tf_op jit(solution)/shard_map/first_step/pallas_call | solution.py:423
  95.7 20.4 %all_to_all.43 = bf16[8,4,64,128]{3,2,1,0:T(8,128)(2,1)S(1)} all-to-all(bf16[8,4,64,128]{3,2,1,0:T(8,128)(2,1)S(1)} %get-tuple-element.55), channel_id=1, replica_groups={{0,1,2,3,4,5,6,7},{8,9,10,11,12,13,14,15},{16,17,18,19,20,21,22,23},{24..., dimensions={0} | all-to-all | bytes 1048576 | tf_op jit(solution)/shard_map/all_to_all | solution.py:72
  117.9 2.4 %collective-permute-start.10 = (bf16[4,4,64,128]{3,2,1,0:T(8,128)(2,1)S(1)}, bf16[4,4,64,128]{3,2,1,0:T(8,128)(2,1)S(1)}, u32[]{:S(2)}, u32[]{:S(2)}) collective-permute-start(bf16[4,4,64,128]{3,2,1,0:T(8,128)(2,1)S(1)} %get-tuple-element.65), channel_id=1, source_target_pairs={{0,24},{1,25},{2,26},{3,27},{4,28},{5,29},{6,30},{7,31},{8,0},{9,1... | collective-permute-start | bytes 786440 | tf_op jit(solution)/shard_map/ppermute | solution.py:78
  120.4 3.4 %copy-done.2 = bf16[4,64,128,128]{3,2,1,0:T(8,128)(2,1)S(1)} copy-done((bf16[4,64,128,128]{3,2,1,0:T(8,128)(2,1)S(1)}, bf16[4,64,128,128]{3,2,1,0:T(8,128)(2,1)}, u32[]{:S(2)}) %copy-start.2) | copy-done | bytes 8388632
  125.5 2.7 %collective-permute-start.9 = (bf16[4,4,64,128]{3,2,1,0:T(8,128)(2,1)S(1)}, bf16[4,4,64,128]{3,2,1,0:T(8,128)(2,1)S(1)}, u32[]{:S(2)}, u32[]{:S(2)}) collective-permute-start(bf16[4,4,64,128]{3,2,1,0:T(8,128)(2,1)S(1)} %collective-permute-done.7), channel_id=1, source_target_pairs={{0,24},{1,25},{2,26},{3,27},{4,28},{5,29},{6,30},{7,31},{8,0},{9,1... | collective-permute-start | bytes 786440 | tf_op jit(solution)/shard_map/ppermute | solution.py:83
  128.3 2.9 %collective-permute-done.11 = bf16[4,4,64,128]{3,2,1,0:T(8,128)(2,1)S(1)} collective-permute-done((bf16[4,4,64,128]{3,2,1,0:T(8,128)(2,1)S(1)}, bf16[4,4,64,128]{3,2,1,0:T(8,128)(2,1)S(1)}, u32[]{:S(2)}, u32[]{:S(2)}) %collective-permute-start.11) | collective-permute-done | bytes 262176 | tf_op jit(solution)/shard_map/ppermute | solution.py:78
  132.9 3.9 %collective-permute-done.8 = bf16[4,4,64,128]{3,2,1,0:T(8,128)(2,1)S(1)} collective-permute-done((bf16[4,4,64,128]{3,2,1,0:T(8,128)(2,1)S(1)}, bf16[4,4,64,128]{3,2,1,0:T(8,128)(2,1)S(1)}, u32[]{:S(2)}, u32[]{:S(2)}) %collective-permute-start.8) | collective-permute-done | bytes 262176 | tf_op jit(solution)/shard_map/ppermute | solution.py:83
  136.8 2.5 %far_tiles.3 = (f32[64,512]{1,0:T(8,128)S(1)}, f32[192,128]{1,0:T(8,128)S(1)}) custom-call(s32[336]{0:T(512)S(1)} %get-tuple-element.40.table, s32[84]{0:T(128)S(1)} %get-tuple-element.41.rows, s32[3]{0:T(128)S(1)} %get-tuple-element.51.totals, bf16[16,64,128]{2,1,0:T(8,128)(2,1)S(1)} %bitcast.49, bf16[16,64,128]{2,1,0:T(8,128)(2,1)S(1)} %bitcast.51, ...), custom_call_target="tpu_custom_call" | custom-call | flops 268435456 | bytes 8388608 | tf_op jit(solution)/shard_map/far_tiles/pallas_call | solution.py:279
  139.3 12.0 %all_to_all.44 = f32[32,8,128]{2,1,0:T(8,128)S(1)} all-to-all(f32[32,8,128]{2,1,0:T(8,128)S(1)} %pad_bitcast_fusion), channel_id=1, replica_groups={{0,32,8,40,16,48,24,56,64,96,72,104,80,112,88,120,128,160,136,168,144,1..., dimensions={0} | all-to-all | bytes 262144 | tf_op jit(solution)/shard_map/all_to_all | solution.py:89
  151.3 9.2 %all_to_all.45 = f32[8,8,128]{2,1,0:T(8,128)S(1)} all-to-all(f32[8,8,128]{2,1,0:T(8,128)S(1)} %broadcast_in_dim.10), channel_id=1, replica_groups={{0,1,2,3,4,5,6,7},{8,9,10,11,12,13,14,15},{16,17,18,19,20,21,22,23},{24..., dimensions={0} | all-to-all | bytes 65536 | tf_op jit(solution)/shard_map/all_to_all | solution.py:47
  160.6 12.4 %all_to_all.46 = f32[32,8,128]{2,1,0:T(8,128)S(1)} all-to-all(f32[32,8,128]{2,1,0:T(8,128)S(1)} %broadcast_in_dim.11), channel_id=1, replica_groups={{0,32,8,40,16,48,24,56,64,96,72,104,80,112,88,120,128,160,136,168,144,1..., dimensions={0} | all-to-all | bytes 262144 | tf_op jit(solution)/shard_map/all_to_all | solution.py:47
  173.0 4.3 %last_step.1 = (f32[2,64,512]{2,1,0:T(8,128)}, f32[2,64,64]{2,1,0:T(8,128)}) custom-call(f32[512,128]{1,0:T(8,128)S(1)} %bitcast.38, f32[256,128]{1,0:T(8,128)S(1)} %bitcast.39, f32[64,256]{1,0:T(8,128)S(1)} %get-tuple-element.61.cross, f32[64,512]{1,0:T(8,128)S(1)} %get-tuple-element.62.product, f32[256,512]{1,0:T(8,128)S(1)} %bitcast.34, ...), custom_call_target="tpu_custom_call" | custom-call | tf_op jit(solution)/shard_map/last_step/pallas_call | solution.py:442
  (51 shorter events, 17.0 us)
Async XLA Ops:
  2.4 27.0 %all-to-all-start = ((bf16[8,4,64,128]{3,2,1,0:T(8,128)(2,1)}), bf16[8,4,64,128]{3,2,1,0:T(8,128)(2,1)S(1)}, u32[]{:S(2)}, u32[]{:S(2)}) async-start(bf16[8,4,64,128]{3,2,1,0:T(8,128)(2,1)} %spread_latest.1), calls=%async_computation | async-start | bytes 1048576 | tf_op jit(solution)/shard_map/all_to_all | solution.py:72
  12.2 0.7 copy-start.4
  29.4 10.8 %collective-permute-start.1 = (bf16[4,4,64,128]{3,2,1,0:T(8,128)(2,1)S(1)}, bf16[4,4,64,128]{3,2,1,0:T(8,128)(2,1)S(1)}, u32[]{:S(2)}, u32[]{:S(2)}) collective-permute-start(bf16[4,4,64,128]{3,2,1,0:T(8,128)(2,1)S(1)} %get-tuple-element.66), channel_id=1, source_target_pairs={{0,24},{1,25},{2,26},{3,27},{4,28},{5,29},{6,30},{7,31},{8,0},{9,1... | collective-permute-start | bytes 786440 | tf_op jit(solution)/shard_map/ppermute | solution.py:77
  32.2 8.3 %collective-permute-start = (bf16[4,4,64,128]{3,2,1,0:T(8,128)(2,1)S(1)}, bf16[4,4,64,128]{3,2,1,0:T(8,128)(2,1)S(1)}, u32[]{:S(2)}, u32[]{:S(2)}) collective-permute-start(bf16[4,4,64,128]{3,2,1,0:T(8,128)(2,1)S(1)} %get-tuple-element.67), channel_id=1, source_target_pairs={{0,8},{1,9},{2,10},{3,11},{4,12},{5,13},{6,14},{7,15},{8,16},{9,17... | collective-permute-start | bytes 786440 | tf_op jit(solution)/shard_map/ppermute | solution.py:77
  32.3 13.8 %collective-permute-start.5 = (bf16[4,4,64,128]{3,2,1,0:T(8,128)(2,1)S(1)}, bf16[4,4,64,128]{3,2,1,0:T(8,128)(2,1)S(1)}, u32[]{:S(2)}, u32[]{:S(2)}) collective-permute-start(bf16[4,4,64,128]{3,2,1,0:T(8,128)(2,1)S(1)} %get-tuple-element.66), channel_id=1, source_target_pairs={{0,8},{1,9},{2,10},{3,11},{4,12},{5,13},{6,14},{7,15},{8,16},{9,17... | collective-permute-start | bytes 786440 | tf_op jit(solution)/shard_map/ppermute | solution.py:78
  32.4 13.7 %collective-permute-start.4 = (bf16[4,4,64,128]{3,2,1,0:T(8,128)(2,1)S(1)}, bf16[4,4,64,128]{3,2,1,0:T(8,128)(2,1)S(1)}, u32[]{:S(2)}, u32[]{:S(2)}) collective-permute-start(bf16[4,4,64,128]{3,2,1,0:T(8,128)(2,1)S(1)} %get-tuple-element.67), channel_id=1, source_target_pairs={{0,24},{1,25},{2,26},{3,27},{4,28},{5,29},{6,30},{7,31},{8,0},{9,1... | collective-permute-start | bytes 786440 | tf_op jit(solution)/shard_map/ppermute | solution.py:78
  35.1 3.4 %copy-start = (bf16[4,64,128,128]{3,2,1,0:T(8,128)(2,1)S(1)}, bf16[4,64,128,128]{3,2,1,0:T(8,128)(2,1)}, u32[]{:S(2)}) copy-start(bf16[4,64,128,128]{3,2,1,0:T(8,128)(2,1)} %param.4) | copy-start | bytes 25165828
  38.5 7.6 %copy-start.1 = (bf16[4,64,128,128]{3,2,1,0:T(8,128)(2,1)S(1)}, bf16[4,64,128,128]{3,2,1,0:T(8,128)(2,1)}, u32[]{:S(2)}) copy-start(bf16[4,64,128,128]{3,2,1,0:T(8,128)(2,1)} %param.4) | copy-start | bytes 25165828
  38.5 13.2 %copy-start.3 = (f32[4,64,512]{2,1,0:T(8,128)S(1)}, f32[4,64,512]{2,1,0:T(8,128)}, u32[]{:S(2)}) copy-start(f32[4,64,512]{2,1,0:T(8,128)} %latest.1) | copy-start | bytes 1572868
  40.5 11.2 %collective-permute-start.2 = (bf16[4,4,64,128]{3,2,1,0:T(8,128)(2,1)S(1)}, bf16[4,4,64,128]{3,2,1,0:T(8,128)(2,1)S(1)}, u32[]{:S(2)}, u32[]{:S(2)}) collective-permute-start(bf16[4,4,64,128]{3,2,1,0:T(8,128)(2,1)S(1)} %collective-permute-done), channel_id=1, source_target_pairs={{0,8},{1,9},{2,10},{3,11},{4,12},{5,13},{6,14},{7,15},{8,16},{9,17... | collective-permute-start | bytes 786440 | tf_op jit(solution)/shard_map/ppermute | solution.py:83
  40.5 11.2 %collective-permute-start.3 = (bf16[4,4,64,128]{3,2,1,0:T(8,128)(2,1)S(1)}, bf16[4,4,64,128]{3,2,1,0:T(8,128)(2,1)S(1)}, u32[]{:S(2)}, u32[]{:S(2)}) collective-permute-start(bf16[4,4,64,128]{3,2,1,0:T(8,128)(2,1)S(1)} %collective-permute-done.1), channel_id=1, source_target_pairs={{0,24},{1,25},{2,26},{3,27},{4,28},{5,29},{6,30},{7,31},{8,0},{9,1... | collective-permute-start | bytes 786440 | tf_op jit(solution)/shard_map/ppermute | solution.py:83
  116.2 9.2 %collective-permute-start.7 = (bf16[4,4,64,128]{3,2,1,0:T(8,128)(2,1)S(1)}, bf16[4,4,64,128]{3,2,1,0:T(8,128)(2,1)S(1)}, u32[]{:S(2)}, u32[]{:S(2)}) collective-permute-start(bf16[4,4,64,128]{3,2,1,0:T(8,128)(2,1)S(1)} %get-tuple-element.64), channel_id=1, source_target_pairs={{0,24},{1,25},{2,26},{3,27},{4,28},{5,29},{6,30},{7,31},{8,0},{9,1... | collective-permute-start | bytes 786440 | tf_op jit(solution)/shard_map/ppermute | solution.py:77
  117.2 8.3 %collective-permute-start.6 = (bf16[4,4,64,128]{3,2,1,0:T(8,128)(2,1)S(1)}, bf16[4,4,64,128]{3,2,1,0:T(8,128)(2,1)S(1)}, u32[]{:S(2)}, u32[]{:S(2)}) collective-permute-start(bf16[4,4,64,128]{3,2,1,0:T(8,128)(2,1)S(1)} %get-tuple-element.65), channel_id=1, source_target_pairs={{0,8},{1,9},{2,10},{3,11},{4,12},{5,13},{6,14},{7,15},{8,16},{9,17... | collective-permute-start | bytes 786440 | tf_op jit(solution)/shard_map/ppermute | solution.py:77
  117.7 13.5 %collective-permute-start.11 = (bf16[4,4,64,128]{3,2,1,0:T(8,128)(2,1)S(1)}, bf16[4,4,64,128]{3,2,1,0:T(8,128)(2,1)S(1)}, u32[]{:S(2)}, u32[]{:S(2)}) collective-permute-start(bf16[4,4,64,128]{3,2,1,0:T(8,128)(2,1)S(1)} %get-tuple-element.64), channel_id=1, source_target_pairs={{0,8},{1,9},{2,10},{3,11},{4,12},{5,13},{6,14},{7,15},{8,16},{9,17... | collective-permute-start | bytes 786440 | tf_op jit(solution)/shard_map/ppermute | solution.py:78
  117.9 13.2 %collective-permute-start.10 = (bf16[4,4,64,128]{3,2,1,0:T(8,128)(2,1)S(1)}, bf16[4,4,64,128]{3,2,1,0:T(8,128)(2,1)S(1)}, u32[]{:S(2)}, u32[]{:S(2)}) collective-permute-start(bf16[4,4,64,128]{3,2,1,0:T(8,128)(2,1)S(1)} %get-tuple-element.65), channel_id=1, source_target_pairs={{0,24},{1,25},{2,26},{3,27},{4,28},{5,29},{6,30},{7,31},{8,0},{9,1... | collective-permute-start | bytes 786440 | tf_op jit(solution)/shard_map/ppermute | solution.py:78
  120.4 3.4 %copy-start.2 = (bf16[4,64,128,128]{3,2,1,0:T(8,128)(2,1)S(1)}, bf16[4,64,128,128]{3,2,1,0:T(8,128)(2,1)}, u32[]{:S(2)}) copy-start(bf16[4,64,128,128]{3,2,1,0:T(8,128)(2,1)} %param.4) | copy-start | bytes 25165828
  125.5 11.2 %collective-permute-start.8 = (bf16[4,4,64,128]{3,2,1,0:T(8,128)(2,1)S(1)}, bf16[4,4,64,128]{3,2,1,0:T(8,128)(2,1)S(1)}, u32[]{:S(2)}, u32[]{:S(2)}) collective-permute-start(bf16[4,4,64,128]{3,2,1,0:T(8,128)(2,1)S(1)} %collective-permute-done.6), channel_id=1, source_target_pairs={{0,8},{1,9},{2,10},{3,11},{4,12},{5,13},{6,14},{7,15},{8,16},{9,17... | collective-permute-start | bytes 786440 | tf_op jit(solution)/shard_map/ppermute | solution.py:83
  125.5 11.2 %collective-permute-start.9 = (bf16[4,4,64,128]{3,2,1,0:T(8,128)(2,1)S(1)}, bf16[4,4,64,128]{3,2,1,0:T(8,128)(2,1)S(1)}, u32[]{:S(2)}, u32[]{:S(2)}) collective-permute-start(bf16[4,4,64,128]{3,2,1,0:T(8,128)(2,1)S(1)} %collective-permute-done.7), channel_id=1, source_target_pairs={{0,24},{1,25},{2,26},{3,27},{4,28},{5,29},{6,30},{7,31},{8,0},{9,1... | collective-permute-start | bytes 786440 | tf_op jit(solution)/shard_map/ppermute | solution.py:83
